TPU v7x, 128 devices: a whole 4x4x4 slice. The times are simulated.
128 devices in a mesh: gx: 8 (over x, core), bulk: 16 (over y, z).
Axes of the slice: x: 4, y: 4, z: 4, core: 2. Of those that a mesh axis runs over, the one named last changes fastest.
Arguments:
- basis: bfloat16 [8, 64, 524288], P(None, None, ('gx', 'bulk')), may hold values from -6 to 6
- near_blocks: bfloat16 [2048, 8, 256, 256], P(('gx', 'bulk')), may hold values from -0.125 to 0.125
- near_src: int32 [2048, 8], P(('gx', 'bulk')), may hold values from 0 to 47
- near_count: int32 [2048], P(('gx', 'bulk')), may hold values from 1 to 8
- p2m: bfloat16 [2048, 256, 128], P(('gx', 'bulk')), may hold values from -0.375 to 0.375
- m2l: bfloat16 [16, 128, 128], replicated, may hold values from -0.25 to 0.25
- send_list: int32 [128, 128, 4], P(('gx', 'bulk')), may hold values from 0 to 15
- send_count: int32 [128, 128], P(('gx', 'bulk')), may hold values from 0 to 4
- far_src: int32 [2048, 32], P(('gx', 'bulk')), may hold values from 0 to 511
- far_class: int32 [2048, 32], P(('gx', 'bulk')), may hold values from 0 to 15
Outputs:
- next_block: bfloat16 [64, 524288], P(None, ('gx', 'bulk'))
- projections: float32 [8, 64, 64], replicated
- factor: float32 [64, 64], replicated
All inputs are finite; a program needn't handle non-finite values.
Results may differ from a plain program's by a relative error of at most 0.012.
Values may be sent and summed in bfloat16 or wider, within the bound.
A program may use at most 128 MiB of HBM per device.

v0:
```python
import jax
import jax.numpy as jnp
from jax import lax
from jax.sharding import Mesh
from jax.sharding import PartitionSpec as P

GX = ("gx_0", "gx_1")
BULK = ("bulk_0", "bulk_1")
GX_BULK = ("gx_0", "gx_1", "bulk_0", "bulk_1")


def extended(array, sides, width):
    for axis, dim in sides:
        devices, length = (lax.axis_size(axis), array.shape[dim])
        up = [(i, (i + 1) % devices) for i in range(devices - 1)]
        down = [(j, i) for i, j in up]
        last = lax.slice_in_dim(array, length - width, length, axis=dim)
        first = lax.slice_in_dim(array, 0, width, axis=dim)
        before = lax.ppermute(last, axis, up)
        after = lax.ppermute(first, axis, down)
        array = jnp.concatenate([before, array, after], axis=dim)
    return array


def filled_up(lines, devices):
    spare = -len(lines) % devices
    return jnp.pad(lines, [(0, spare)] + [(0, 0)] * (lines.ndim - 1))


def from_everyone(array, axis):
    copies = jnp.broadcast_to(array, (lax.axis_size(axis), *array.shape))
    return lax.all_to_all(copies, axis, split_axis=0, concat_axis=0, tiled=True)


def joined_along(pieces, dim):
    dims = list(pieces.shape[1:])
    dims[dim] *= pieces.shape[0]
    return jnp.moveaxis(pieces, 0, dim).reshape(dims)


def gathered_by_axis(array, axes, dim):
    far, near = axes
    first = from_everyone(array, far)
    pieces = jnp.swapaxes(from_everyone(first, near), 0, 1)
    return joined_along(pieces.reshape(-1, *array.shape), dim)


def in_blocks(array, dim, devices):
    dims = array.shape
    pieces = array.reshape(*dims[:dim], devices, dims[dim] // devices, *dims[dim + 1 :])
    return jnp.moveaxis(pieces, dim, 0)


def sent_and_summed(array, axis, dim):
    pieces = in_blocks(array, dim, lax.axis_size(axis))
    arrived = lax.all_to_all(pieces, axis, split_axis=0, concat_axis=0, tiled=True)
    return arrived.sum(axis=0)


def sum_by_axis(array, axes, dim):
    far, near = axes
    pieces = in_blocks(array, dim, lax.axis_size(far))
    nearer = sent_and_summed(pieces, near, dim + 1)
    arrived = lax.all_to_all(nearer, far, split_axis=0, concat_axis=0, tiled=True)
    return arrived.sum(axis=0)


def sum_by_parts(array, axes):
    padded = filled_up(array, lax.axis_size(axes[0]) * lax.axis_size(axes[1]))
    whole = gathered_by_axis(sum_by_axis(padded, axes, 0), axes, 0)
    return lax.slice_in_dim(whole, 0, len(array)).reshape(array.shape)


def together(arrays, axis):
    flat, at, gathered = (jnp.concatenate([a.reshape(-1) for a in arrays]), 0, [])
    total = sum_by_parts(flat, axis)
    for a in arrays:
        gathered.append(total[at : at + a.size].reshape(a.shape))
        at += a.size
    return tuple(gathered)


def split_parts(values):
    upper = values.astype(jnp.bfloat16)
    lower = (values - upper.astype(jnp.float32)).astype(jnp.bfloat16)
    return (upper, lower)


def basis_times(basis, image):
    upper, lower = split_parts(image)
    first = jnp.einsum("krn,sn->krs", basis, upper, preferred_element_type=jnp.float32)
    second = jnp.einsum("krn,sn->krs", basis, lower, preferred_element_type=jnp.float32)
    return first + second


def combine_basis(projections, basis):
    upper, lower = split_parts(projections)
    first = jnp.einsum("krs,krn->sn", upper, basis, preferred_element_type=jnp.float32)
    second = jnp.einsum("krs,krn->sn", lower, basis, preferred_element_type=jnp.float32)
    return first + second


def shards(
    basis, near_blocks, near_src, near_count, p2m, m2l, send_list, send_count, far_src, far_class
):
    blocks, rhs_count, columns = basis.shape
    leaves, slots_near = near_src.shape
    panels = near_blocks.shape[2]
    terms = p2m.shape[2]
    classes = m2l.shape[0]
    col_groups = lax.axis_size(GX)
    segments = lax.axis_size(BULK)
    peers = col_groups * segments
    slot_count = send_list.shape[2]
    total_rows = columns * peers
    source = basis[blocks - 1].reshape(rhs_count, leaves, panels)
    padded = extended(source, ((GX, 1),), leaves)
    picked = jnp.take(padded, near_src.reshape(-1), axis=1).reshape(
        rhs_count, leaves, slots_near, panels
    )
    live = (lax.broadcasted_iota(jnp.int32, (leaves, slots_near), 1) < near_count[:, None]).astype(
        jnp.bfloat16
    )
    picked = picked * live[None, :, :, None]
    near = jnp.einsum("rlkq,lkpq->rlp", picked, near_blocks, preferred_element_type=jnp.float32)
    mult = jnp.einsum("rlp,lpq->lrq", source, p2m, preferred_element_type=jnp.float32).astype(
        jnp.bfloat16
    )
    outgoing = jnp.take(mult, send_list[0].reshape(-1), axis=0).reshape(
        peers, slot_count, rhs_count, terms
    )
    filled = (
        lax.broadcasted_iota(jnp.int32, (peers, slot_count), 1) < send_count[0][:, None]
    ).astype(jnp.bfloat16)
    outgoing = outgoing * filled[:, :, None, None]
    received = lax.all_to_all(outgoing, GX_BULK, split_axis=0, concat_axis=0, tiled=True)
    flat = received.reshape(peers * slot_count, rhs_count, terms)
    sources = jnp.take(flat, far_src.reshape(-1), axis=0).reshape(leaves, -1, rhs_count, terms)
    onehot = (far_class[:, :, None] == lax.broadcasted_iota(jnp.int32, (1, 1, classes), 2)).astype(
        jnp.bfloat16
    )
    gathered = jnp.einsum(
        "lec,lerq->clrq", onehot, sources, preferred_element_type=jnp.float32
    ).astype(jnp.bfloat16)
    local = jnp.einsum("clrq,cqs->lrs", gathered, m2l, preferred_element_type=jnp.float32).astype(
        jnp.bfloat16
    )
    far = jnp.einsum("lrq,lpq->rlp", local, p2m, preferred_element_type=jnp.float32)
    image = (source.astype(jnp.float32) + near + far).reshape(rhs_count, columns)
    highest = lax.Precision.HIGHEST
    inner_vw = basis_times(basis, image)
    inner_ww = jnp.dot(image, image.T, precision=highest)
    inner_vv = jnp.einsum("jrn,ksn->jkrs", basis, basis, preferred_element_type=jnp.float32)
    sum_vw, sum_ww, sum_vv = together(
        (inner_vw, inner_ww, inner_vv), (("gx_0", "gx_1", "bulk_0"), "bulk_1")
    )
    projections = sum_vw / total_rows
    basis_gram = sum_vv / total_rows
    resid = image - combine_basis(projections, basis)
    twice = jnp.einsum("krs,krt->st", projections, projections, precision=highest)
    mixed = jnp.einsum("jrs,jkrt,ktu->su", projections, basis_gram, projections, precision=highest)
    gram = sum_ww / total_rows - 2.0 * twice + mixed
    factor = jnp.linalg.cholesky(gram)
    next_block = lax.linalg.triangular_solve(factor, resid, left_side=True, lower=True).astype(
        jnp.bfloat16
    )
    return (next_block, projections, factor)


def solution(mesh):
    finer = Mesh(mesh.devices.reshape(4, 2, 4, 4), ("gx_0", "gx_1", "bulk_0", "bulk_1"))
    in_specs = (
        P(None, None, GX_BULK),
        P(GX_BULK, None, None, None),
        P(GX_BULK, None),
        P(GX_BULK),
        P(GX_BULK, None, None),
        P(),
        P(GX_BULK, None, None),
        P(GX_BULK, None),
        P(GX_BULK, None),
        P(GX_BULK, None),
    )
    out_specs = (P(None, GX_BULK), P(), P())
    return jax.shard_map(
        shards, mesh=finer, in_specs=in_specs, out_specs=out_specs, check_vma=False
    )
```

profile of v0, /device:TPU:1, one launch (start us, length us, event | category | flops | bytes accessed | tf_op | source)
XLA Modules:
  0.0 321.0 jit_solution(12877078102955733821)
XLA Ops:
  4.8 13.5 %gather_fusion.1 = bf16[512,64,128]{2,1,0:T(8,128)(2,1)} fusion(bf16[16,64,128]{2,1,0:T(8,128)(2,1)S(1)} %convolution_convert_fusion.1, s32[1024]{0:T(1024)S(1)} %pad_clamp_fusion.1), kind=kCustom, calls=%fused_computation.1 | custom fusion | bytes 16779264 | tf_op jit(solution)/shard_map/jit(_take)/gather | solution.py:129
  18.3 7.4 %select_multiply_fusion = bf16[128,4,64,128]{3,2,1,0:T(8,128)(2,1)} fusion(bf16[128,4,64,128]{3,2,1,0:T(8,128)(2,1)} %bitcast.128, pred[128,4]{1,0:T(8,128)(4,1)S(1)} %copy.110, bf16[128,4]{1,0:T(8,128)(2,1)S(1)} %fusion.57), kind=kLoop, calls=%fused_computation.5 | loop fusion | flops 8388608 | bytes 16778752 | tf_op jit(solution)/shard_map/mul | solution.py:135
  25.7 11.9 %all-to-all-start = ((bf16[128,4,64,128]{3,2,1,0:T(8,128)(2,1)}), bf16[128,4,64,128]{3,2,1,0:T(8,128)(2,1)}, u32[]{:S(2)}, u32[]{:S(2)}) async-start(bf16[128,4,64,128]{3,2,1,0:T(8,128)(2,1)} %select_multiply_fusion), calls=%async_computation | async-start | bytes 16777216 | tf_op jit(solution)/shard_map/all_to_all | solution.py:136
  38.6 3.0 collective-permute-start.1
  44.7 9.1 %fusion.17 = f32[8,8,64,64]{2,3,0,1:T(8,128)} fusion(bf16[8,64,4096]{2,1,0:T(8,128)(2,1)} %param.10), kind=kOutput, calls=%fused_computation.24 | convolution fusion | flops 2147483648 | bytes 5242880 | tf_op jit(solution)/shard_map/jrn,ksn->jkrs/dot_general | solution.py:153
  57.2 84.6 %collective-permute-done.1 = bf16[64,16,256]{2,0,1:T(8,128)(2,1)} collective-permute-done((bf16[64,16,256]{2,0,1:T(8,128)(2,1)}, bf16[64,16,256]{2,0,1:T(8,128)(2,1)}, u32[]{:S(2)}, u32[]{:S(2)}) %collective-permute-start.1) | collective-permute-done | bytes 524320 | tf_op jit(solution)/shard_map/ppermute | solution.py:20
  143.4 2.8 gather_fusion
  146.1 23.0 %gather_fusion.2 = bf16[512,64,128]{2,1,0:T(8,128)(2,1)} fusion(bf16[512,64,128]{2,1,0:T(8,128)(2,1)} %bitcast.10, s32[1024]{0:T(1024)S(1)} %pad_clamp_fusion), kind=kCustom, calls=%fused_computation.2 | custom fusion | bytes 16779264 | tf_op jit(solution)/shard_map/jit(_take)/gather | solution.py:138
  169.2 4.7 %broadcast_select_fusion = bf16[16,32,64,128]{3,2,1,0:T(8,128)(2,1)S(1)} fusion(bf16[16,32,64,128]{3,2,1,0:T(8,128)(2,1)} %bitcast.129, pred[16,32]{1,0:T(8,128)(4,1)S(1)} %compare_and_fusion), kind=kLoop, calls=%fused_computation.6 | loop fusion | flops 4194304 | bytes 16777728 | tf_op jit(solution)/shard_map/jit(_take)/select_n | solution.py:138
  173.9 7.1 %convert_bitcast_fusion = bf16[16,16,64,128]{3,0,2,1:T(8,128)(2,1)} fusion(bf16[16,32,64,128]{3,2,1,0:T(8,128)(2,1)S(1)} %broadcast_select_fusion, s32[16,32]{1,0:T(8,128)S(1)} %copy-done.11), kind=kOutput, calls=%fused_computation.17 | convolution fusion | flops 136323072 | bytes 12584960 | tf_op jit(solution)/shard_map/lec,lerq->clrq/dot_general | solution.py:142
  181.0 4.3 %convolution_bitcast_fusion.2 = f32[64,16,256]{2,0,1:T(8,128)S(1)} fusion(bf16[16,256,128]{2,1,0:T(8,128)(2,1)S(1)} %copy-done, bf16[16,16,64,128]{3,0,2,1:T(8,128)(2,1)} %convert_bitcast_fusion, bf16[16,128,128]{2,1,0:T(8,128)(2,1)} %param.15), kind=kOutput, calls=%fused_computation.27 | convolution fusion | flops 604110848 | bytes 6815744 | tf_op jit(solution)/shard_map/lrq,lpq->rlp/dot_general | solution.py:148
  185.4 10.0 %fusion.31 = f32[64,16,256]{2,0,1:T(8,128)S(1)} fusion(f32[64,16,256]{2,0,1:T(8,128)S(1)} %convolution_bitcast_fusion.2, bf16[16,8,256,256]{3,2,1,0:T(8,128)(2,1)} %param.11, bf16[64,16,8,256]{3,0,2,1:T(8,128)(2,1)} %bitcast.139, pred[16,8]{1,0:T(8,128)(4,1)S(1)} %copy.105, bf16[16,8]{1,0:T(8,128)(2,1)S(1)} %fusion.60, bf16[64,16,256]{2,1,0:T(8,128)(2,1)S(1)} %bitcast.138), kind=kOutput, calls=%fused_computation.30 | convolution fusion | flops 1078722560 | bytes 23593344 | tf_op jit(solution)/shard_map/rlkq,lkpq->rlp/dot_general | solution.py:125
  196.5 4.5 %fusion.45 = f32[64,8,64]{2,0,1:T(8,128)S(1)} fusion(bf16[8,64,4096]{2,1,0:T(8,128)(2,1)} %param.10, f32[64,4096]{1,0:T(8,128)S(1)} %bitcast.130), kind=kOutput, calls=%fused_computation.46 | convolution fusion | flops 268697600 | bytes 5373952 | tf_op jit(solution)/shard_map/krn,sn->krs/dot_general | solution.py:91
  201.0 2.8 fusion.39
  210.0 23.9 %all_to_all.33 = f32[4,32,2336]{2,1,0:T(8,128)S(1)} all-to-all(f32[4,32,2336]{2,1,0:T(8,128)S(1)} %copy.118), channel_id=1, replica_groups=mesh['gx_0'=4,'gx_1'=2,'bulk_0'=4,'bulk_1'=4] {'bulk_1'}, dimensions={0} | all-to-all | bytes 2392064 | tf_op jit(solution)/shard_map/all_to_all | solution.py:56
  235.9 14.6 %all_to_all.34 = f32[32,1,2336]{2,1,0:T(1,128)S(1)} all-to-all(f32[32,1,2336]{2,1,0:T(1,128)S(1)} %all_to_all.23), channel_id=1, replica_groups=mesh['gx_0'=4,'gx_1'=2,'bulk_0'=4,'bulk_1'=4] {'gx_0','gx_1','bulk_0'}, dimensions={0} | all-to-all | bytes 598016 | tf_op jit(solution)/shard_map/all_to_all | solution.py:64
  250.9 13.2 %all_to_all.35 = f32[32,1,2336]{2,1,0:T(1,128)S(1)} all-to-all(f32[32,1,2336]{2,1,0:T(1,128)S(1)} %broadcast_in_dim.48), channel_id=1, replica_groups=mesh['gx_0'=4,'gx_1'=2,'bulk_0'=4,'bulk_1'=4] {'gx_0','gx_1','bulk_0'}, dimensions={0} | all-to-all | bytes 598016 | tf_op jit(solution)/shard_map/all_to_all | solution.py:32
  264.2 19.6 %all_to_all.36 = f32[4,32,2336]{2,1,0:T(8,128)S(1)} all-to-all(f32[4,32,2336]{2,1,0:T(8,128)S(1)} %broadcast_in_dim.49), channel_id=1, replica_groups=mesh['gx_0'=4,'gx_1'=2,'bulk_0'=4,'bulk_1'=4] {'bulk_1'}, dimensions={0} | all-to-all | bytes 2392064 | tf_op jit(solution)/shard_map/all_to_all | solution.py:32
  284.6 3.2 slice.31
  289.7 3.2 slice.29
  294.1 3.4 %convolution_bitcast_fusion.1 = f32[64,4096]{1,0:T(8,128)S(1)} fusion(bf16[8,64,4096]{2,1,0:T(8,128)(2,1)} %param.10, f32[8,64,64]{2,1,0:T(8,128)S(1)} %slice_multiply_fusion.1), kind=kOutput, calls=%fused_computation.10 | convolution fusion | flops 268468224 | bytes 5373952 | tf_op jit(solution)/shard_map/krs,krn->sn/dot_general | solution.py:98
  305.0 5.8 %cholesky.16 = f32[64,64]{1,0:T(8,128)S(1)} custom-call(f32[64,64]{1,0:T(8,128)S(1)} %fusion.59), custom_call_target="Cholesky" | custom-call | tf_op jit(solution)/shard_map/jit(cholesky)/cholesky | solution.py:163
  312.8 4.9 %custom-call.6 = f32[1,64,64]{1,2,0:T(8,128)S(1)} custom-call(f32[1,64,64]{2,1,0:T(8,128)S(1)} %get-tuple-element.3), custom_call_target="InvertDiagBlocksLowerTriangular" | custom-call | tf_op jit(solution)/shard_map/triangular_solve | solution.py:164
  317.7 3.1 convolution_convert_fusion
  (83 shorter events, 36.1 us)
Async XLA Ops:
  0.6 3.8 %copy-start = (bf16[16,256,128]{2,1,0:T(8,128)(2,1)S(1)}, bf16[16,256,128]{2,1,0:T(8,128)(2,1)}, u32[]{:S(2)}) copy-start(bf16[16,256,128]{2,1,0:T(8,128)(2,1)} %param.14) | copy-start | bytes 3145732
  3.4 34.2 %copy-start.4 = (bf16[8,8,16,256]{3,2,1,0:T(8,128)(2,1)}, bf16[8,8,16,256]{3,2,1,0:T(8,128)(2,1)S(1)}, u32[]{:S(2)}) copy-start(bf16[8,8,16,256]{3,2,1,0:T(8,128)(2,1)S(1)} %copy.150) | copy-start | bytes 1572868
  25.7 18.7 %copy-start.8 = (s32[16,32]{1,0:T(8,128)S(1)}, s32[16,32]{1,0:T(8,128)}, u32[]{:S(2)}) copy-start(s32[16,32]{1,0:T(8,128)} %param.18) | copy-start | bytes 6148
  25.7 18.8 %copy-start.9 = (s32[16,8]{0,1:T(8,128)S(1)}, s32[16,8]{0,1:T(8,128)}, u32[]{:S(2)}) copy-start(s32[16,8]{0,1:T(8,128)} %param.12) | copy-start | bytes 1540
  25.7 120.5 %all-to-all-start = ((bf16[128,4,64,128]{3,2,1,0:T(8,128)(2,1)}), bf16[128,4,64,128]{3,2,1,0:T(8,128)(2,1)}, u32[]{:S(2)}, u32[]{:S(2)}) async-start(bf16[128,4,64,128]{3,2,1,0:T(8,128)(2,1)} %select_multiply_fusion), calls=%async_computation | async-start | bytes 16777216 | tf_op jit(solution)/shard_map/all_to_all | solution.py:136
  38.6 103.3 %collective-permute-start.1 = (bf16[64,16,256]{2,0,1:T(8,128)(2,1)}, bf16[64,16,256]{2,0,1:T(8,128)(2,1)}, u32[]{:S(2)}, u32[]{:S(2)}) collective-permute-start(bf16[64,16,256]{2,0,1:T(8,128)(2,1)} %copy.104), channel_id=1, source_target_pairs={{16,0},{32,16},{48,32},{64,48},{80,64},{96,80},{112,96},{17,1},{33... | collective-permute-start | bytes 1572872 | tf_op jit(solution)/shard_map/ppermute | solution.py:20
  41.6 100.2 %collective-permute-start = (bf16[64,16,256]{2,0,1:T(8,128)(2,1)}, bf16[64,16,256]{2,0,1:T(8,128)(2,1)}, u32[]{:S(2)}, u32[]{:S(2)}) collective-permute-start(bf16[64,16,256]{2,0,1:T(8,128)(2,1)} %copy.104), channel_id=1, source_target_pairs={{0,16},{16,32},{32,48},{48,64},{64,80},{80,96},{96,112},{1,17},{17... | collective-permute-start | bytes 1572872 | tf_op jit(solution)/shard_map/ppermute | solution.py:19
  53.8 3.3 %copy-start.10 = (s32[16]{0:T(128)S(1)}, s32[16]{0:T(128)}, u32[]{:S(2)}) copy-start(s32[16]{0:T(128)} %param.13) | copy-start | bytes 196
  169.2 4.8 %copy-start.11 = (s32[16,32]{1,0:T(8,128)S(1)}, s32[16,32]{1,0:T(8,128)}, u32[]{:S(2)}) copy-start(s32[16,32]{1,0:T(8,128)} %param.19) | copy-start | bytes 6148
  181.0 4.3 %copy-start.5 = (bf16[8,8,16,256]{3,2,1,0:T(8,128)(2,1)S(1)}, bf16[8,8,16,256]{3,2,1,0:T(8,128)(2,1)}, u32[]{:S(2)}) copy-start(bf16[8,8,16,256]{3,2,1,0:T(8,128)(2,1)} %copy-done.4) | copy-start | bytes 1572868
  196.5 4.5 %copy-start.1 = (bf16[8,64,4096]{2,1,0:T(8,128)(2,1)S(1)}, bf16[8,64,4096]{2,1,0:T(8,128)(2,1)}, u32[]{:S(2)}) copy-start(bf16[8,64,4096]{2,1,0:T(8,128)(2,1)} %param.10) | copy-start | bytes 12582916
  201.0 5.7 %copy-start.7 = (f32[262144]{0:T(1024)S(1)}, f32[262144]{0:T(1024)}, u32[]{:S(2)}) copy-start(f32[262144]{0:T(1024)} %reshape.212) | copy-start | bytes 3145732
  292.9 4.5 %copy-start.2 = (bf16[8,64,4096]{2,1,0:T(8,128)(2,1)S(1)}, bf16[8,64,4096]{2,1,0:T(8,128)(2,1)}, u32[]{:S(2)}) copy-start(bf16[8,64,4096]{2,1,0:T(8,128)(2,1)} %param.10) | copy-start | bytes 12582916
  294.0 10.3 %copy-start.3 = (f32[8,64,64]{2,1,0:T(8,128)}, f32[8,64,64]{2,1,0:T(8,128)S(1)}, u32[]{:S(2)}) copy-start(f32[8,64,64]{2,1,0:T(8,128)S(1)} %slice_multiply_fusion.1) | copy-start | bytes 393220
  297.4 1.9 copy-start.6
  299.3 4.9 %slice-start = ((f32[4672,64]{1,0:T(8,128)}), f32[64,64]{1,0:T(8,128)S(1)}, s32[]{:S(2)}) async-start(f32[4672,64]{1,0:T(8,128)} %slice.29), calls=%async_computation.5 | async-start | bytes 65536 | tf_op jit(solution)/shard_map/slice | solution.py:78
where the time goes:
time: 327 us; the launch traced here: 321 us
  waiting for transfers between devices  84.6 us (26%)
  blocking collectives  71.3 us (22%)
  local copies, waits for them, and re-layouts  63.8 us (20%)
  matrix products  50.1 us (15%)
  other arithmetic  32.2 us (10%)
  starting transfers between devices  17.7 us (5%)
    ppermute x1, waiting for transfers between devices, extended(): after = lax.ppermute(first, axis, down)  84.6 us
    all_to_all x2, blocking collectives, from_everyone(): return lax.all_to_all(copies, axis, split_axis=0, concat_axis=0, tiled=True)  32.8 us
    all_to_all x1, blocking collectives, sent_and_summed(): lax.all_to_all(pieces, axis, split_axis=0, concat_axis=0, tiled=True)  23.9 us
    gather x1, local copies, waits for them, and re-layouts, shards(): jnp.take(flat, far_src.reshape(-1), axis=0)  23 us
    all_to_all x1, blocking collectives, sum_by_axis(): lax.all_to_all(nearer, far, split_axis=0, concat_axis=0, tiled=True)  14.6 us
    gather x1, local copies, waits for them, and re-layouts, shards(): jnp.take(mult, send_list[0].reshape(-1), axis=0)  13.5 us
    all_to_all x1, starting transfers between devices, shards(): lax.all_to_all(outgoing, GX_BULK, split_axis=0, concat_axis=0, tiled=True)  11.9 us
    dot_general x1, matrix products, shards(): jnp.einsum('rlkq,lkpq->rlp', picked, near_blocks, preferred_element_type=...  9.98 us
  transfers between devices with their start and end apart: 3, of which 1 were waited for; matrix products, arithmetic and copies ran while one was open for 6% of the time, Pallas kernels for 0%

commit v1 on v0

v1 whole, which is shorter than its diff:
```python
import functools

import jax
import jax.numpy as jnp
from jax import lax
from jax.experimental import pallas as pl
from jax.experimental.pallas import tpu as pltpu
from jax.sharding import Mesh
from jax.sharding import PartitionSpec as P

ALL = ("x", "c", "y", "z")
ORDERS = (("x", "y", "z"), ("y", "z", "x"), ("z", "x", "y"))
MESH = pl.DeviceIdType.MESH
F32, BF16 = jnp.float32, jnp.bfloat16
LIMIT = 67043328
EXTRA = 16
NT = (((1,), (1,)), ((), ()))
TN = (((0,), (0,)), ((), ()))


def dot(a, b, dims=(((1,), (0,)), ((), ()))):
    return lax.dot_general(a, b, dims, preferred_element_type=F32)


def halves(values):
    upper = values.astype(BF16)
    return upper, (values - upper.astype(F32)).astype(BF16)


def mult_kernel(per_step, rhs, x_ref, p_ref, list_ref, count_ref, out_ref, leaf_ref):
    step = pl.program_id(0)
    panels = p_ref.shape[1]
    for i in range(per_step):
        vector = x_ref[0, :, i * panels : (i + 1) * panels]
        leaf_ref[i] = vector
        block = dot(vector, p_ref[i]).astype(BF16)
        at = pl.multiple_of((step * per_step + i) * rhs, rhs)
        out_ref[pl.ds(at, rhs), :] = block

    @pl.when(step == 0)
    def _():
        peers, slots = list_ref.shape[1:]
        widen = (
            lax.broadcasted_iota(jnp.int32, (slots, EXTRA), 0)
            == lax.broadcasted_iota(jnp.int32, (slots, EXTRA), 1)
        ).astype(BF16)
        eye = (
            lax.broadcasted_iota(jnp.int32, (peers, peers), 0)
            == lax.broadcasted_iota(jnp.int32, (peers, peers), 1)
        ).astype(BF16)
        wide = dot(list_ref[0].astype(F32).astype(BF16), widen).astype(BF16)
        table = dot(wide, eye, TN)
        counts = jnp.broadcast_to(count_ref[...].astype(F32), (EXTRA, peers))
        row = lax.broadcasted_iota(jnp.int32, (EXTRA, peers), 0)
        rows = out_ref.shape[0]
        out_ref[rows - EXTRA : rows, :] = jnp.where(row == slots, counts, table).astype(BF16)


def multipoles(basis, p2m, send_list, send_count):
    blocks, rhs, columns = basis.shape
    leaves, panels, terms = p2m.shape
    steps = 4
    per = leaves // steps
    rows = leaves * rhs + EXTRA
    return pl.pallas_call(
        functools.partial(mult_kernel, per, rhs),
        grid=(steps,),
        in_specs=[
            pl.BlockSpec((1, rhs, per * panels), lambda i: (blocks - 1, 0, i)),
            pl.BlockSpec((per, panels, terms), lambda i: (i, 0, 0)),
            pl.BlockSpec(send_list.shape, lambda i: (0, 0, 0)),
            pl.BlockSpec(send_count.shape, lambda i: (0, 0)),
        ],
        out_specs=(
            pl.BlockSpec((rows, terms), lambda i: (0, 0)),
            pl.BlockSpec((per, rhs, panels), lambda i: (i, 0, 0)),
        ),
        out_shape=(
            jax.ShapeDtypeStruct((rows, terms), BF16),
            jax.ShapeDtypeStruct((leaves, rhs, panels), BF16),
        ),
        name="multipoles",
    )(basis, p2m, send_list, send_count)


def spread_kernel(
    cuts, mult_ref, x_ref, near_blocks_ref, src_ref, live_ref,
    all_ref, base_ref,
    xbuf, nbuf, send_sem, recv_sem, sib_send, sib_recv, halo_send, halo_recv, own_sem, x_sem, nsem,
):
    me = {name: lax.axis_index(name) for name in ALL}
    leaves = near_blocks_ref.shape[0]
    slots = near_blocks_ref.shape[1]
    panels = near_blocks_ref.shape[2]
    depth = nbuf.shape[0]
    column = me["x"] * 2 + me["c"]

    def at(axis, by):
        return lax.rem(me[axis] + (by + 4), 4)

    def near_copy(leaf, slot):
        return pltpu.make_async_copy(near_blocks_ref.at[leaf], nbuf.at[slot], nsem.at[slot])

    own_x = pltpu.make_async_copy(x_ref, xbuf.at[pl.ds(leaves, leaves)], x_sem)
    own_x.start()
    for leaf in range(depth):
        near_copy(leaf, leaf).start()

    other = {"c": 1 - me["c"]}
    barrier = pltpu.get_barrier_semaphore()
    peers = [{axis: at(axis, by)} for axis in ("x", "y", "z") for by in (1, -1)]
    peers.append(other)
    gx = 8
    after_col = lax.rem(column + 1, gx)
    before_col = lax.rem(column + gx - 1, gx)
    after = {"x": after_col // 2, "c": lax.rem(after_col, 2)}
    before = {"x": before_col // 2, "c": lax.rem(before_col, 2)}
    peers += [after, before]
    for peer in peers:
        pl.semaphore_signal(barrier, inc=1, device_id=peer, device_id_type=MESH)
    pl.semaphore_wait(barrier, len(peers))

    def place(where, rows, core):
        index = []
        for name in ALL:
            if name == "c":
                index.append(core)
            elif name in where:
                index.append(where[name])
            else:
                index.append(slice(None))
        return all_ref.at[tuple(index) + (pl.ds(rows[0], rows[1] - rows[0]),)]

    units = [(0, None, None)]
    units += [(1, r, None) for r in (0, -1, 1, 2)]
    units += [(2, r, 0) for r in (0, -1, 1, 2)]
    units += [(2, None, r) for r in (-1, 1, 2)]
    number = {u: i for i, u in enumerate(units)}
    started = []

    def where_of(colour, unit, by):
        axes = ORDERS[colour]
        phase, first, second = unit
        where = {}
        if phase == 0:
            where = {axes[0]: by, axes[1]: 0, axes[2]: 0}
        elif phase == 1:
            where = {axes[0]: first, axes[1]: by, axes[2]: 0}
        else:
            where = {axes[1]: second, axes[2]: by}
            if first is not None:
                where[axes[0]] = first
        return where

    def rows_of(colour, part):
        low, high = cuts[colour], cuts[colour + 1]
        middle = low + (high - low) // 32 * 16
        return {"all": (low, high), "lower": (low, middle), "upper": (middle, high)}[part]

    def remote(colour, unit, kind):
        axis = ORDERS[colour][unit[0]]
        by, to, part = ((0, 1, "all"), (0, -1, "all"), (-1, 1, "lower"), (1, -1, "upper"))[kind]
        offsets = where_of(colour, unit, by)
        where = {name: at(name, v) for name, v in offsets.items()}
        rows = rows_of(colour, part)
        dst = place(where, rows, me["c"])
        src = dst
        if len(offsets) == 3 and all(v == 0 for v in offsets.values()):
            src = mult_ref.at[pl.ds(rows[0], rows[1] - rows[0])]
        i = number[unit]
        return pltpu.make_async_remote_copy(
            src_ref=src,
            dst_ref=dst,
            send_sem=send_sem.at[colour, i, kind],
            recv_sem=recv_sem.at[colour, i, kind],
            device_id={axis: at(axis, to)},
            device_id_type=MESH,
        )

    def send(colour, unit):
        for kind in (0, 1):
            copy = remote(colour, unit, kind)
            copy.start()
            started.append(copy)

    def arrived(colour, unit):
        for kind in (0, 1):
            remote(colour, unit, kind).wait_recv()
        for kind in (2, 3):
            copy = remote(colour, unit, kind)
            copy.start()
            started.append(copy)

    def arrived_far(colour, unit):
        for kind in (2, 3):
            remote(colour, unit, kind).wait_recv()

    crossings = []

    def cross(colour, second, third):
        axes = ORDERS[colour]
        where = {axes[1]: at(axes[1], second), axes[2]: at(axes[2], third)}
        ref = place(where, rows_of(colour, "all"), me["c"])
        i = ((0, -1, 1, 2).index(second)) * 4 + (0, -1, 1, 2).index(third)
        copy = pltpu.make_async_remote_copy(
            src_ref=ref,
            dst_ref=ref,
            send_sem=sib_send.at[colour, i],
            recv_sem=sib_recv.at[colour, i],
            device_id=other,
            device_id_type=MESH,
        )
        copy.start()
        other_ref = place(where, rows_of(colour, "all"), other["c"])
        arrival = pltpu.make_async_remote_copy(
            src_ref=other_ref,
            dst_ref=other_ref,
            send_sem=sib_send.at[colour, i],
            recv_sem=sib_recv.at[colour, i],
            device_id=other,
            device_id_type=MESH,
        )
        crossings.append((copy, arrival))

    done_leaves = [0]

    def near(count):
        first = done_leaves[0]
        last = min(leaves, first + count)
        done_leaves[0] = last
        if last == first:
            return
        if first == 0:
            own_x.wait()
            for copy in halo:
                copy.wait_recv()

            @pl.when(column == 0)
            def _():
                xbuf[:leaves] = jnp.zeros((leaves,) + xbuf.shape[1:], BF16)

            @pl.when(column == gx - 1)
            def _():
                xbuf[2 * leaves :] = jnp.zeros((leaves,) + xbuf.shape[1:], BF16)

        def body(leaf, carry):
            slot = lax.rem(leaf, depth)
            near_copy(leaf, slot).wait()
            lanes = pl.ds(pl.multiple_of(leaf * panels, panels), panels)
            total = xbuf[leaves + leaf].astype(F32)
            for k in range(slots):
                i = leaf * slots + k
                total = total + live_ref[i] * dot(xbuf[src_ref[i]], nbuf[slot, k], NT)
            base_ref[:, lanes] = total

            @pl.when(leaf + depth < leaves)
            def _():
                near_copy(leaf + depth, slot).start()

            return carry

        lax.fori_loop(first, last, body, 0)

    colours = range(3)
    for unit in (units[0], (1, 0, None), (2, 0, 0)):
        for k in colours:
            send(k, unit)
    keep = pltpu.make_async_copy(
        mult_ref, all_ref.at[me["x"], me["c"], me["y"], me["z"]], own_sem
    )
    keep.start()
    halo = []
    for i, (target, slot) in enumerate(((after, 0), (before, 2))):
        copy = pltpu.make_async_remote_copy(
            src_ref=x_ref,
            dst_ref=xbuf.at[pl.ds(slot * leaves, leaves)],
            send_sem=halo_send.at[i],
            recv_sem=halo_recv.at[i],
            device_id=target,
            device_id_type=MESH,
        )
        copy.start()
        halo.append(copy)

    for k in colours:
        arrived(k, units[0])
        for r in (-1, 1):
            send(k, (1, r, None))
    for k in colours:
        arrived_far(k, units[0])
        send(k, (1, 2, None))
    for k in colours:
        arrived(k, (1, 0, None))
        for r in (-1, 1, 2):
            send(k, (2, r, 0))
    keep.wait()
    for k in colours:
        cross(k, 0, 0)
    for r in (-1, 1, 2):
        for k in colours:
            arrived(k, (1, r, None))
    for k in colours:
        arrived(k, (2, 0, 0))
    for r in (-1, 1):
        for k in colours:
            send(k, (2, None, r))
    for r in (0, -1, 1, 2):
        for k in colours:
            arrived_far(k, (1, r, None))
    for k in colours:
        send(k, (2, None, 2))
    for r in (-1, 1, 2):
        for k in colours:
            cross(k, r, 0)
    near(1)
    for r in (-1, 1, 2):
        for k in colours:
            arrived(k, (2, r, 0))
        near(1)
    for k in colours:
        for t in (-1, 1):
            cross(k, 0, t)
    near(1)
    for r in (-1, 1):
        for k in colours:
            arrived(k, (2, None, r))
            for t in (-1, 1):
                cross(k, r, t)
            near(1)
    for r in (0, -1, 1, 2):
        for k in colours:
            arrived_far(k, (2, r, 0))
        near(1)
    for k in colours:
        cross(k, 0, 2)
    near(leaves)
    for k in colours:
        arrived(k, (2, None, 2))
        for t in (-1, 1):
            cross(k, 2, t)
    for r in (-1, 1, 2):
        for k in colours:
            arrived_far(k, (2, None, r))
            cross(k, r, 2)
    for copy, arrival in crossings:
        arrival.wait_recv()
    for copy, arrival in crossings:
        copy.wait_send()
    for copy in started:
        copy.wait_send()
    for copy in halo:
        copy.wait_send()


def spread(mult, x, near_blocks, near_src, near_count):
    rows, terms = mult.shape
    leaves, slots, panels, _ = near_blocks.shape
    rhs = x.shape[1]
    live = lax.broadcasted_iota(jnp.int32, (leaves, slots), 1) < near_count[:, None]
    tiles = rows // 16
    cuts = (0, 23 * 16, 43 * 16, tiles * 16)
    depth = 4
    hbm = pl.BlockSpec(memory_space=pl.ANY)
    vmem = pl.BlockSpec(memory_space=pltpu.VMEM)
    smem = pl.BlockSpec(memory_space=pltpu.SMEM)
    dma = pltpu.SemaphoreType.DMA
    return pl.pallas_call(
        functools.partial(spread_kernel, cuts),
        in_specs=[vmem, hbm, hbm, smem, smem],
        out_specs=(hbm, vmem),
        out_shape=(
            jax.ShapeDtypeStruct((4, 2, 4, 4, rows, terms), BF16),
            jax.ShapeDtypeStruct((rhs, leaves * panels), F32),
        ),
        scratch_shapes=[
            pltpu.VMEM((3 * leaves, rhs, panels), BF16),
            pltpu.VMEM((depth, slots, panels, panels), BF16),
            dma((3, 12, 4)), dma((3, 12, 4)), dma((3, 16)), dma((3, 16)),
            dma((2,)), dma((2,)), dma, dma, dma((depth,)),
        ],
        compiler_params=pltpu.CompilerParams(
            collective_id=0, has_side_effects=True, vmem_limit_bytes=32 << 20
        ),
        name="spread",
    )(mult, x, near_blocks, near_src.reshape(-1), live.astype(F32).reshape(-1))


def far_kernel(
    src_ref, class_ref, table_ref, all_ref, base_ref, p_ref, m2l_ref, basis_ref,
    image_ref, inner_ref,
    buf, acc, grouped, vbuf, sems, vsem,
):
    leaves, panels, terms = p_ref.shape
    rhs = base_ref.shape[0]
    slots = src_ref.shape[0] // leaves
    classes = m2l_ref.shape[0] // terms
    blocks = basis_ref.shape[0]
    ahead = 4
    group = grouped.shape[0] // rhs

    def entry(i):
        f = src_ref[i]
        sender = f // 4
        leaf = table_ref[sender * 8 + (f - sender * 4)]
        return sender, leaf

    def fetch(leaf):
        def one(e, carry):
            i = leaf * slots + e
            sender, at = entry(i)
            rows = pl.ds(pl.multiple_of(at * rhs, rhs), rhs)
            pltpu.make_async_copy(all_ref.at[sender, rows], buf.at[i], sems.at[leaf]).start()
            return carry

        lax.fori_loop(0, slots, one, 0, unroll=8)

    whole = pltpu.make_async_copy(basis_ref, vbuf, vsem)
    for leaf in range(ahead):
        fetch(leaf)
    whole.start()
    inner_ref[...] = jnp.zeros_like(inner_ref)

    def per_group(g, carry):
        def per_leaf(j, carry):
            leaf = g * group + j

            @pl.when(leaf + ahead < leaves)
            def _():
                fetch(leaf + ahead)

            view = buf.at[pl.ds(leaf * slots, slots)]
            pltpu.make_async_copy(view, view, sems.at[leaf]).wait()
            acc[...] = jnp.zeros_like(acc)

            def one(e, carry):
                i = leaf * slots + e
                f = src_ref[i]
                sender = f // 4
                valid = (f - sender * 4) < table_ref[sender * 8 + 4]
                which = jnp.where(valid, class_ref[i], classes)
                acc[which] += buf[i].astype(F32)
                return carry

            lax.fori_loop(0, slots, one, 0, unroll=8)
            at = pl.ds(pl.multiple_of(j * rhs, rhs), rhs)
            for c in range(classes):
                grouped[at, c * terms : (c + 1) * terms] = acc[c].astype(BF16)
            return carry

        lax.fori_loop(0, group, per_leaf, 0)
        local = dot(grouped[...], m2l_ref[...]).astype(BF16)

        @pl.when(g == 0)
        def _():
            whole.wait()

        for j in range(group):
            leaf = g * group + j
            lanes = pl.ds(pl.multiple_of(leaf * panels, panels), panels)
            far = dot(local[j * rhs : (j + 1) * rhs], p_ref[leaf], NT)
            image = base_ref[:, lanes] + far
            image_ref[:, lanes] = image
            both = jnp.concatenate(halves(image), axis=0)
            v = vbuf[:, :, lanes].reshape(blocks * rhs, panels)
            out = dot(both, v, NT)
            inner_ref[...] += out[:rhs] + out[rhs:]
        return carry

    lax.fori_loop(0, leaves // group, per_group, 0)


def far_field(far_src, far_class, table, everyone, base, p2m, m2l, basis):
    leaves, panels, terms = p2m.shape
    blocks, rhs, columns = basis.shape
    slots = far_src.shape[1]
    classes = m2l.shape[0]
    hbm = pl.BlockSpec(memory_space=pl.ANY)
    vmem = pl.BlockSpec(memory_space=pltpu.VMEM)
    smem = pl.BlockSpec(memory_space=pltpu.SMEM)
    dma = pltpu.SemaphoreType.DMA
    group = 4
    return pl.pallas_call(
        far_kernel,
        in_specs=[smem, smem, smem, hbm, vmem, vmem, vmem, hbm],
        out_specs=(vmem, vmem),
        out_shape=(
            jax.ShapeDtypeStruct((rhs, columns), F32),
            jax.ShapeDtypeStruct((rhs, blocks * rhs), F32),
        ),
        scratch_shapes=[
            pltpu.VMEM((leaves * slots, rhs, terms), BF16),
            pltpu.VMEM((classes + 1, rhs, terms), F32),
            pltpu.VMEM((group * rhs, classes * terms), BF16),
            pltpu.VMEM((blocks, rhs, columns), BF16),
            dma((leaves,)), dma,
        ],
        compiler_params=pltpu.CompilerParams(vmem_limit_bytes=40 << 20),
        name="far_field",
    )(
        far_src.reshape(-1), far_class.reshape(-1), table, everyone, base, p2m,
        m2l.reshape(classes * terms, terms), basis,
    )


def finish_kernel(
    total_rows, inner_ref, image_ref, basis_ref,
    next_ref, proj_ref, factor_ref,
    vbuf, gram_in, one_in, two_in, stack, piece, whole, gone, two_gone,
    s1, r1, s2, r2, s3, r3, vsem,
):
    me = {name: lax.axis_index(name) for name in ALL}
    column = me["x"] * 2 + me["c"]
    segment = me["y"] * 4 + me["z"]
    gx, bulk = 8, 16
    rhs, columns = image_ref.shape
    blocks = basis_ref.shape[0]
    load = pltpu.make_async_copy(basis_ref, vbuf, vsem)
    load.start()

    def col_peer(by):
        c = lax.rem(column + by, gx)
        return c, {"x": c // 2, "c": lax.rem(c, 2)}

    def seg_peer(by):
        s = lax.rem(segment + by, bulk)
        return s, {"y": s // 4, "z": lax.rem(s, 4)}

    barrier = pltpu.get_barrier_semaphore()
    for by in range(1, gx):
        pl.semaphore_signal(barrier, inc=1, device_id=col_peer(by)[1], device_id_type=MESH)
    for by in range(1, bulk):
        pl.semaphore_signal(barrier, inc=1, device_id=seg_peer(by)[1], device_id_type=MESH)
    pl.semaphore_wait(barrier, gx + bulk - 2)

    def remote(src, dst, send, recv, peer):
        return pltpu.make_async_remote_copy(
            src_ref=src, dst_ref=dst, send_sem=send, recv_sem=recv,
            device_id=peer, device_id_type=MESH,
        )

    def all_reduce(n, source, arrivals, mine, parts, result):
        rows = rhs // gx
        sent = []
        for by in range(1, gx):
            c, peer = col_peer(by)
            at = pl.ds(pl.multiple_of(c * rows, rows), rows)
            copy = remote(source.at[at], arrivals.at[gx - by], s1.at[n, by], r1.at[n, gx - by], peer)
            copy.start()
            sent.append(copy)
        own = pl.ds(pl.multiple_of(column * rows, rows), rows)
        total = source[own, :]
        for by in range(1, gx):
            remote(arrivals.at[by], arrivals.at[by], s1.at[n, by], r1.at[n, by], col_peer(1)[1]).wait_recv()
            total = total + arrivals[by]
        mine[...] = total
        for by in range(1, bulk):
            s, peer = seg_peer(by)
            copy = remote(mine, parts.at[segment], s2.at[n, by], r2.at[n, bulk - by], peer)
            copy.start()
            sent.append(copy)
        parts[segment] = total
        for by in range(1, bulk):
            s, peer = seg_peer(by)
            remote(mine, parts.at[s], s2.at[n, by], r2.at[n, by], peer).wait_recv()
        total = parts[0]
        for s in range(1, bulk):
            total = total + parts[s]
        result[own, :] = total
        for by in range(1, gx):
            c, peer = col_peer(by)
            copy = remote(result.at[own], result.at[own], s3.at[n, by], r3.at[n, gx - by], peer)
            copy.start()
            sent.append(copy)
        for by in range(1, gx):
            c, peer = col_peer(by)
            at = pl.ds(pl.multiple_of(c * rows, rows), rows)
            remote(result.at[at], result.at[at], s3.at[n, by], r3.at[n, by], peer).wait_recv()
        for copy in sent:
            copy.wait_send()

    scale = 1.0 / total_rows
    all_reduce(0, inner_ref, one_in, piece, two_in, whole)
    load.wait()
    proj = whole[...] * scale
    coef = jnp.concatenate(halves(proj), axis=0)
    step = 512
    gram = jnp.zeros((2 * rhs, 2 * rhs), F32)
    for i in range(0, columns, step):
        v = vbuf[:, :, i : i + step].reshape(blocks * rhs, step)
        out = dot(coef, v)
        resid = image_ref[:, i : i + step] - (out[:rhs] + out[rhs:])
        both = jnp.concatenate(halves(resid), axis=0)
        stack[:, i : i + step] = both
        gram = gram + dot(both, both, NT)
    gram_in[...] = gram[:rhs] + gram[rhs:]
    for i in range(0, blocks * rhs, 2 * rhs):
        proj_ref[i : i + 2 * rhs, :] = proj[:, i : i + 2 * rhs].T
    all_reduce(1, gram_in, gone, piece.at[:, : 2 * rhs], two_gone, factor_ref)
    folded = factor_ref[...] * scale
    folded = folded + pltpu.roll(folded, rhs, 1)
    lane = lax.broadcasted_iota(jnp.int32, (rhs, 2 * rhs), 1)
    row = lax.broadcasted_iota(jnp.int32, (rhs, 2 * rhs), 0)
    work = jnp.where(lane < rhs, folded, (lane - rhs == row).astype(F32))
    tall = 8
    count = rhs // tall
    part = [work[i * tall : (i + 1) * tall] for i in range(count)]
    low = lax.broadcasted_iota(jnp.int32, (tall, 2 * rhs), 0)
    for b in range(count):
        cols = [
            {i: jnp.broadcast_to(part[i][:, b * tall + t : b * tall + t + 1], (tall, 2 * rhs)) for i in range(b, count)}
            for t in range(tall)
        ]
        for t in range(tall):
            inverse = 1.0 / cols[t][b][t : t + 1, :]
            across = {u: cols[u][b][t : t + 1, :] * inverse for u in range(t + 1, tall)}
            pivot = part[b][t : t + 1, :] * inverse
            for i in range(b, count):
                factor = cols[t][i]
                if i == b:
                    factor = jnp.where(low > t, factor, 0.0)
                part[i] = part[i] - factor * pivot
                for u in range(t + 1, tall):
                    cols[u][i] = cols[u][i] - factor * across[u]
    work = jnp.concatenate(part, axis=0)
    diagonal = jnp.sum(jnp.where(lane == row, work, 0.0), axis=1, keepdims=True)
    work = work * lax.rsqrt(diagonal)
    factor_ref[...] = jnp.where((lane >= row) & (lane < rhs), work, 0.0)
    right = jnp.where(lane < rhs, 0.0, work)
    right = right + pltpu.roll(right, rhs, 1)
    left = jnp.concatenate(halves(right), axis=0)
    for i in range(0, columns, step):
        out = dot(left, stack[:, i : i + step])
        next_ref[:, i : i + step] = (out[:rhs] + out[rhs:]).astype(BF16)


def finish(inner, image, basis, total_rows):
    blocks, rhs, columns = basis.shape
    wide = blocks * rhs
    hbm = pl.BlockSpec(memory_space=pl.ANY)
    vmem = pl.BlockSpec(memory_space=pltpu.VMEM)
    dma = pltpu.SemaphoreType.DMA
    return pl.pallas_call(
        functools.partial(finish_kernel, total_rows),
        in_specs=[vmem, vmem, hbm],
        out_specs=(vmem, vmem, vmem),
        out_shape=(
            jax.ShapeDtypeStruct((rhs, columns), BF16),
            jax.ShapeDtypeStruct((wide, rhs), F32),
            jax.ShapeDtypeStruct((rhs, 2 * rhs), F32),
        ),
        scratch_shapes=[
            pltpu.VMEM((blocks, rhs, columns), BF16),
            pltpu.VMEM((rhs, 2 * rhs), F32),
            pltpu.VMEM((8, 8, wide), F32),
            pltpu.VMEM((16, 8, wide), F32),
            pltpu.VMEM((2 * rhs, columns), BF16),
            pltpu.VMEM((8, wide), F32),
            pltpu.VMEM((rhs, wide), F32),
            pltpu.VMEM((8, 8, 2 * rhs), F32),
            pltpu.VMEM((16, 8, 2 * rhs), F32),
            dma((2, 8)), dma((2, 8)), dma((2, 16)), dma((2, 16)), dma((2, 8)), dma((2, 8)), dma,
        ],
        compiler_params=pltpu.CompilerParams(
            collective_id=1, has_side_effects=True, vmem_limit_bytes=32 << 20
        ),
        name="finish",
    )(inner, image, basis)


def shards(
    basis, near_blocks, near_src, near_count, p2m, m2l, send_list, send_count, far_src, far_class
):
    blocks, rhs, columns = basis.shape
    leaves, panels, terms = p2m.shape
    peers = lax.axis_size(ALL)
    slots = send_list.shape[2]
    mult, x = multipoles(basis, p2m, send_list, send_count)
    everyone, base = spread(mult, x, near_blocks, near_src, near_count)
    everyone = everyone.reshape(peers, *mult.shape)
    rows = leaves * rhs
    lists = lax.slice(everyone, (0, rows, 0), (peers, rows + 8, terms))
    me = lax.axis_index(ALL)
    table = lax.dynamic_slice_in_dim(lists, me, 1, axis=2).astype(jnp.int32).reshape(-1)
    image, inner = far_field(far_src, far_class, table, everyone, base, p2m, m2l, basis)
    new, proj, upper = finish(inner, image, basis, columns * peers)
    factor = upper[:, :rhs].T
    return (new, proj.reshape(blocks, rhs, rhs), factor)


def solution(mesh):
    finer = Mesh(mesh.devices.reshape(4, 2, 4, 4), ALL)
    in_specs = (
        P(None, None, ALL),
        P(ALL, None, None, None),
        P(ALL, None),
        P(ALL),
        P(ALL, None, None),
        P(),
        P(ALL, None, None),
        P(ALL, None),
        P(ALL, None),
        P(ALL, None),
    )
    out_specs = (P(None, ALL), P(), P())
    return jax.shard_map(
        shards, mesh=finer, in_specs=in_specs, out_specs=out_specs, check_vma=False
    )
```

time: 327 us -> 163 us (0.50); the launches traced: 321 us -> 163 us
  Pallas kernels: 0 us -> 142 us
  waiting for transfers between devices: 84.6 us -> 0 us
  blocking collectives: 71.3 us -> 0 us
  matrix products: 50.1 us -> 0 us
  local copies, waits for them, and re-layouts: 63.8 us -> 17.2 us
  other arithmetic: 32.2 us -> 3.06 us
  starting transfers between devices: 17.7 us -> 0 us
    pallas_call x0 -> x4, Pallas kernels: none -> 142 us  [the longest x1 84.7 us: spread(): pl.pallas_call(functools.partial(spread_kernel, cuts), in_specs=[vmem, hb...]
    ppermute x2 -> x0, waiting for transfers between devices: 84.6 us -> none  [the longest x1 84.6 us: extended(): after = lax.ppermute(first, axis, down)]
    all_to_all x4 -> x0, blocking collectives: 71.3 us -> none  [the longest x2 32.8 us: from_everyone(): return lax.all_to_all(copies, axis, split_axis=0, concat_axis=0, tiled=True)]
    dot_general x13 -> x0, matrix products: 47.1 us -> none  [the longest x1 9.98 us: shards(): jnp.einsum('rlkq,lkpq->rlp', picked, near_blocks, preferred_element_type=...]
    gather x3 -> x0, local copies, waits for them, and re-layouts: 39.2 us -> none  [the longest x1 23 us: shards(): jnp.take(flat, far_src.reshape(-1), axis=0)]
    unnamed x29 -> x17, local copies, waits for them, and re-layouts: 1.2 us -> 14.3 us
    another operation x5 -> x0, other arithmetic: 12.7 us -> none  [the longest x3 6.52 us: shards(): factor = jnp.linalg.cholesky(gram)]
    all_to_all x1 -> x0, starting transfers between devices: 11.9 us -> none  [shards(): lax.all_to_all(outgoing, GX_BULK, split_axis=0, concat_axis=0, tiled=True)]
  transfers between devices with their start and end apart: 3 -> 0, of which waited for: 1 -> 0; matrix products, arithmetic and copies ran while one was open for 6% -> 0% of each run, Pallas kernels for 0% -> 0%
where the time goes in v1:
time: 163 us
  Pallas kernels  142 us (87%)
  local copies, waits for them, and re-layouts  17.2 us (11%)
  other arithmetic  3.06 us (2%)
    pallas_call x1, Pallas kernels, spread(): pl.pallas_call(functools.partial(spread_kernel, cuts), in_specs=[vmem, hb...  84.7 us
    pallas_call x1, Pallas kernels, finish(): pl.pallas_call(functools.partial(finish_kernel, total_rows), in_specs=[vm...  36 us
    pallas_call x1, Pallas kernels, far_field(): pl.pallas_call(far_kernel, in_specs=[smem, smem, smem, hbm, vmem, vmem, v...  17 us
    unnamed x17, local copies, waits for them, and re-layouts  14.3 us
    pallas_call x1, Pallas kernels, multipoles(): pl.pallas_call(functools.partial(mult_kernel, per, rhs), grid=(steps,), i...  4.11 us

profile of v1, /device:TPU:1, one launch (start us, length us, event | category | flops | bytes accessed | tf_op | source)
XLA Modules:
  0.0 162.8 jit_solution(2905352162751892807)
XLA Ops:
  0.6 0.0 copy-start.2
  0.6 0.0 copy-start.3
  0.7 0.9 reshape.36.src_ref
  1.6 0.8 reshape.37.class_ref
  2.3 0.8 copy.17
  3.1 0.1 reshape.38.src_ref
  3.2 0.7 fusion
  3.9 0.1 reshape.44.live_ref
  4.0 1.4 copy.16.list_ref
  5.4 4.1 %multipoles.1 = (bf16[1040,128]{1,0:T(8,128)(2,1)}, bf16[16,64,256]{2,1,0:T(8,128)(2,1)}) custom-call(bf16[8,64,4096]{2,1,0:T(8,128)(2,1)} %basis_ref.3, bf16[16,256,128]{2,1,0:T(8,128)(2,1)} %p_ref.3, s32[1,128,4]{2,1,0:T(8,128)} %copy.16.list_ref, s32[1,128]{1,0:T(1,128)} %count_ref.1), custom_call_target="tpu_custom_call" | custom-call | tf_op jit(solution)/shard_map/multipoles/pallas_call | solution.py:65
  9.5 5.8 %copy-done.1 = bf16[16,8,256,256]{3,2,1,0:T(8,128)(2,1)S(1)} copy-done((bf16[16,8,256,256]{3,2,1,0:T(8,128)(2,1)S(1)}, bf16[16,8,256,256]{3,2,1,0:T(8,128)(2,1)}, u32[]{:S(2)}) %copy-start.1) | copy-done | bytes 16777240
  15.3 1.0 copy-done.4
  16.3 0.9 copy-done.5
  17.3 84.7 %spread.1 = (bf16[4,2,4,4,1040,128]{5,4,3,2,1,0:T(8,128)(2,1)}, f32[64,4096]{1,0:T(8,128)S(1)}) custom-call(bf16[1040,128]{1,0:T(8,128)(2,1)S(1)} %copy-done.5, bf16[16,64,256]{2,1,0:T(8,128)(2,1)S(1)} %copy-done.4, bf16[16,8,256,256]{3,2,1,0:T(8,128)(2,1)S(1)} %copy-done.1, s32[128]{0:T(128)S(1)} %reshape.38.src_ref, f32[128]{0:T(128)S(1)} %reshape.44.live_ref), custom_call_target="tpu_custom_call" | custom-call | tf_op jit(solution)/shard_map/spread/pallas_call | solution.py:367
  102.0 1.0 slice.8
  102.9 2.3 %convert_reduce_fusion = s32[128,8]{1,0:T(8,128)S(1)} fusion(bf16[128,8,128]{2,1,0:T(8,128)(2,1)S(1)} %slice.8, s32[]{:T(128)S(6)} %select_n.3), kind=kLoop, calls=%fused_computation | loop fusion | flops 1024 | bytes 6148 | tf_op jit(solution)/shard_map/reshape | solution.py:683
  105.3 0.1 reshape.46.table_ref
  105.4 0.0 copy-start
  105.4 2.2 %copy-done = bf16[8,64,4096]{2,1,0:T(8,128)(2,1)S(1)} copy-done((bf16[8,64,4096]{2,1,0:T(8,128)(2,1)S(1)}, bf16[8,64,4096]{2,1,0:T(8,128)(2,1)}, u32[]{:S(2)}) %copy-start) | copy-done | bytes 4194328
  107.6 17.0 %far_field.1 = (f32[64,4096]{1,0:T(8,128)S(1)}, f32[64,512]{1,0:T(8,128)S(1)}) custom-call(s32[512]{0:T(512)S(1)} %reshape.36.src_ref, s32[512]{0:T(512)S(1)} %reshape.37.class_ref, s32[1024]{0:T(1024)S(1)} %reshape.46.table_ref, bf16[128,1040,128]{2,1,0:T(8,128)(2,1)} %bitcast.8, f32[64,4096]{1,0:T(8,128)S(1)} %get-tuple-element.15.base_ref, ...), custom_call_target="tpu_custom_call" | custom-call | tf_op jit(solution)/shard_map/far_field/pallas_call | solution.py:482
  124.6 36.0 %finish.1 = (bf16[64,4096]{1,0:T(8,128)(2,1)S(1)}, f32[512,64]{1,0:T(8,128)S(1)}, f32[64,128]{1,0:T(8,128)S(1)}) custom-call(f32[64,512]{1,0:T(8,128)S(1)} %get-tuple-element.16.inner_ref, f32[64,4096]{1,0:T(8,128)S(1)} %get-tuple-element.17.image_ref, bf16[8,64,4096]{2,1,0:T(8,128)(2,1)S(1)} %copy-done), custom_call_target="tpu_custom_call" | custom-call | tf_op jit(solution)/shard_map/finish/pallas_call | solution.py:642
  160.6 0.7 copy.18
  161.3 0.8 copy.21
  162.1 0.7 copy.22
  (6 shorter events, 0.0 us)
Async XLA Ops:
  0.6 104.7 %copy-start.2 = (bf16[16,256,128]{2,1,0:T(8,128)(2,1)S(1)}, bf16[16,256,128]{2,1,0:T(8,128)(2,1)}, u32[]{:S(2)}) copy-start(bf16[16,256,128]{2,1,0:T(8,128)(2,1)} %p_ref.3) | copy-start | bytes 3145732
  0.6 104.7 %copy-start.3 = (bf16[16,128,128]{2,1,0:T(8,128)(2,1)S(1)}, bf16[16,128,128]{2,1,0:T(8,128)(2,1)}, u32[]{:S(2)}) copy-start(bf16[16,128,128]{2,1,0:T(8,128)(2,1)} %param.15) | copy-start | bytes 1572868
  9.5 5.8 %copy-start.1 = (bf16[16,8,256,256]{3,2,1,0:T(8,128)(2,1)S(1)}, bf16[16,8,256,256]{3,2,1,0:T(8,128)(2,1)}, u32[]{:S(2)}) copy-start(bf16[16,8,256,256]{3,2,1,0:T(8,128)(2,1)} %near_blocks_ref.1) | copy-start | bytes 50331652
  15.3 1.0 copy-start.4
  16.3 1.0 copy-start.5
  105.4 2.2 %copy-start = (bf16[8,64,4096]{2,1,0:T(8,128)(2,1)S(1)}, bf16[8,64,4096]{2,1,0:T(8,128)(2,1)}, u32[]{:S(2)}) copy-start(bf16[8,64,4096]{2,1,0:T(8,128)(2,1)} %basis_ref.3) | copy-start | bytes 12582916

commit v2 on v1

--- a/solution.py
+++ b/solution.py
@@ -13,7 +13,6 @@
 MESH = pl.DeviceIdType.MESH
 F32, BF16 = jnp.float32, jnp.bfloat16
 LIMIT = 67043328
-EXTRA = 16
 NT = (((1,), (1,)), ((), ()))
 TN = (((0,), (0,)), ((), ()))
 
@@ -27,66 +26,12 @@
     return upper, (values - upper.astype(F32)).astype(BF16)
 
 
-def mult_kernel(per_step, rhs, x_ref, p_ref, list_ref, count_ref, out_ref, leaf_ref):
-    step = pl.program_id(0)
-    panels = p_ref.shape[1]
-    for i in range(per_step):
-        vector = x_ref[0, :, i * panels : (i + 1) * panels]
-        leaf_ref[i] = vector
-        block = dot(vector, p_ref[i]).astype(BF16)
-        at = pl.multiple_of((step * per_step + i) * rhs, rhs)
-        out_ref[pl.ds(at, rhs), :] = block
-
-    @pl.when(step == 0)
-    def _():
-        peers, slots = list_ref.shape[1:]
-        widen = (
-            lax.broadcasted_iota(jnp.int32, (slots, EXTRA), 0)
-            == lax.broadcasted_iota(jnp.int32, (slots, EXTRA), 1)
-        ).astype(BF16)
-        eye = (
-            lax.broadcasted_iota(jnp.int32, (peers, peers), 0)
-            == lax.broadcasted_iota(jnp.int32, (peers, peers), 1)
-        ).astype(BF16)
-        wide = dot(list_ref[0].astype(F32).astype(BF16), widen).astype(BF16)
-        table = dot(wide, eye, TN)
-        counts = jnp.broadcast_to(count_ref[...].astype(F32), (EXTRA, peers))
-        row = lax.broadcasted_iota(jnp.int32, (EXTRA, peers), 0)
-        rows = out_ref.shape[0]
-        out_ref[rows - EXTRA : rows, :] = jnp.where(row == slots, counts, table).astype(BF16)
-
-
-def multipoles(basis, p2m, send_list, send_count):
-    blocks, rhs, columns = basis.shape
-    leaves, panels, terms = p2m.shape
-    steps = 4
-    per = leaves // steps
-    rows = leaves * rhs + EXTRA
-    return pl.pallas_call(
-        functools.partial(mult_kernel, per, rhs),
-        grid=(steps,),
-        in_specs=[
-            pl.BlockSpec((1, rhs, per * panels), lambda i: (blocks - 1, 0, i)),
-            pl.BlockSpec((per, panels, terms), lambda i: (i, 0, 0)),
-            pl.BlockSpec(send_list.shape, lambda i: (0, 0, 0)),
-            pl.BlockSpec(send_count.shape, lambda i: (0, 0)),
-        ],
-        out_specs=(
-            pl.BlockSpec((rows, terms), lambda i: (0, 0)),
-            pl.BlockSpec((per, rhs, panels), lambda i: (i, 0, 0)),
-        ),
-        out_shape=(
-            jax.ShapeDtypeStruct((rows, terms), BF16),
-            jax.ShapeDtypeStruct((leaves, rhs, panels), BF16),
-        ),
-        name="multipoles",
-    )(basis, p2m, send_list, send_count)
-
-
 def spread_kernel(
-    cuts, mult_ref, x_ref, near_blocks_ref, src_ref, live_ref,
-    all_ref, base_ref,
-    xbuf, nbuf, send_sem, recv_sem, sib_send, sib_recv, halo_send, halo_recv, own_sem, x_sem, nsem,
+    cuts, basis_ref, p_ref, near_blocks_ref, list_ref, count_ref, src_ref, near_count_ref,
+    all_ref, base_ref, table_ref,
+    xbuf, nbuf, pbuf, mbuf, stage, lists,
+    send_sem, recv_sem, sib_send, sib_recv, halo_send, halo_recv, list_send, list_recv,
+    own_sem, x_sem, p_sem, stage_sem, nsem,
 ):
     me = {name: lax.axis_index(name) for name in ALL}
     leaves = near_blocks_ref.shape[0]
@@ -101,8 +46,14 @@
     def near_copy(leaf, slot):
         return pltpu.make_async_copy(near_blocks_ref.at[leaf], nbuf.at[slot], nsem.at[slot])
 
-    own_x = pltpu.make_async_copy(x_ref, xbuf.at[pl.ds(leaves, leaves)], x_sem)
-    own_x.start()
+    blocks, rhs = basis_ref.shape[:2]
+    mine = xbuf.at[pl.ds(leaves, leaves)]
+    for leaf in range(leaves):
+        pltpu.make_async_copy(
+            basis_ref.at[blocks - 1, :, pl.ds(leaf * panels, panels)], mine.at[leaf], x_sem
+        ).start()
+    load_p = pltpu.make_async_copy(p_ref, pbuf, p_sem)
+    load_p.start()
     for leaf in range(depth):
         near_copy(leaf, leaf).start()
 
@@ -115,9 +66,28 @@
     before_col = lax.rem(column + gx - 1, gx)
     after = {"x": after_col // 2, "c": lax.rem(after_col, 2)}
     before = {"x": before_col // 2, "c": lax.rem(before_col, 2)}
-    peers += [after, before]
+    peers += [after, before] + [{axis: at(axis, 2)} for axis in ("x", "y", "z")]
     for peer in peers:
         pl.semaphore_signal(barrier, inc=1, device_id=peer, device_id_type=MESH)
+    slots_out = list_ref.shape[1]
+    stage[...] = jnp.zeros_like(stage)
+    stage[:slots_out, :] = list_ref[0]
+    stage[slots_out : slots_out + 1, :] = count_ref[...]
+    pltpu.make_async_copy(mine, mine, x_sem).wait()
+    load_p.wait()
+
+    def multipole(leaf, carry):
+        rows = pl.ds(pl.multiple_of(leaf * rhs, rhs), rhs)
+        mbuf[rows, :] = dot(xbuf[leaves + leaf], pbuf[leaf]).astype(BF16)
+        return carry
+
+    lax.fori_loop(0, leaves, multipole, 0, unroll=4)
+    here = all_ref.at[me["x"], me["c"], me["y"], me["z"]]
+    keep = pltpu.make_async_copy(mbuf, here, own_sem)
+    keep.start()
+    my_list = lists.at[me["x"], me["c"], me["y"], me["z"]]
+    keep_list = pltpu.make_async_copy(stage, my_list, stage_sem)
+    keep_list.start()
     pl.semaphore_wait(barrier, len(peers))
 
     def place(where, rows, core):
@@ -164,12 +134,9 @@
         where = {name: at(name, v) for name, v in offsets.items()}
         rows = rows_of(colour, part)
         dst = place(where, rows, me["c"])
-        src = dst
-        if len(offsets) == 3 and all(v == 0 for v in offsets.values()):
-            src = mult_ref.at[pl.ds(rows[0], rows[1] - rows[0])]
         i = number[unit]
         return pltpu.make_async_remote_copy(
-            src_ref=src,
+            src_ref=dst,
             dst_ref=dst,
             send_sem=send_sem.at[colour, i, kind],
             recv_sem=recv_sem.at[colour, i, kind],
@@ -231,7 +198,6 @@
         if last == first:
             return
         if first == 0:
-            own_x.wait()
             for copy in halo:
                 copy.wait_recv()
 
@@ -249,8 +215,8 @@
             lanes = pl.ds(pl.multiple_of(leaf * panels, panels), panels)
             total = xbuf[leaves + leaf].astype(F32)
             for k in range(slots):
-                i = leaf * slots + k
-                total = total + live_ref[i] * dot(xbuf[src_ref[i]], nbuf[slot, k], NT)
+                live = lax.min(lax.max(near_count_ref[leaf] - k, 0), 1).astype(F32)
+                total = total + live * dot(xbuf[src_ref[k, leaf]], nbuf[slot, k], NT)
             base_ref[:, lanes] = total
 
             @pl.when(leaf + depth < leaves)
@@ -261,18 +227,52 @@
 
         lax.fori_loop(first, last, body, 0)
 
+    def list_region(stage_index):
+        index = [me["x"], me["c"], me["y"], me["z"]]
+        for place_of in ((), (0,), (0, 2), (0, 2, 3))[stage_index]:
+            index[place_of] = slice(None)
+        return lists.at[tuple(index)]
+
+    def list_copies(i):
+        if i == 3:
+            targets = [other]
+        else:
+            axis = ("x", "y", "z")[i]
+            targets = [{axis: at(axis, by)} for by in (1, 2, 3)]
+        region = list_region(i)
+        out = []
+        for t, target in enumerate(targets):
+            out.append(
+                pltpu.make_async_remote_copy(
+                    src_ref=region, dst_ref=region,
+                    send_sem=list_send.at[i, t], recv_sem=list_recv.at[i, t],
+                    device_id=target, device_id_type=MESH,
+                )
+            )
+        return out
+
+    list_sent = []
+
+    def lists_go(i):
+        for copy in list_copies(i):
+            copy.start()
+            list_sent.append(copy)
+
+    def lists_come(i):
+        for copy in list_copies(i):
+            copy.wait_recv()
+
     colours = range(3)
+    keep.wait()
+    keep_list.wait()
+    lists_go(0)
     for unit in (units[0], (1, 0, None), (2, 0, 0)):
         for k in colours:
             send(k, unit)
-    keep = pltpu.make_async_copy(
-        mult_ref, all_ref.at[me["x"], me["c"], me["y"], me["z"]], own_sem
-    )
-    keep.start()
     halo = []
     for i, (target, slot) in enumerate(((after, 0), (before, 2))):
         copy = pltpu.make_async_remote_copy(
-            src_ref=x_ref,
+            src_ref=mine,
             dst_ref=xbuf.at[pl.ds(slot * leaves, leaves)],
             send_sem=halo_send.at[i],
             recv_sem=halo_recv.at[i],
@@ -293,9 +293,10 @@
         arrived(k, (1, 0, None))
         for r in (-1, 1, 2):
             send(k, (2, r, 0))
-    keep.wait()
     for k in colours:
         cross(k, 0, 0)
+    lists_come(0)
+    lists_go(1)
     for r in (-1, 1, 2):
         for k in colours:
             arrived(k, (1, r, None))
@@ -312,11 +313,15 @@
     for r in (-1, 1, 2):
         for k in colours:
             cross(k, r, 0)
+    lists_come(1)
+    lists_go(2)
     near(1)
     for r in (-1, 1, 2):
         for k in colours:
             arrived(k, (2, r, 0))
         near(1)
+    lists_come(2)
+    lists_go(3)
     for k in colours:
         for t in (-1, 1):
             cross(k, 0, t)
@@ -334,6 +339,12 @@
     for k in colours:
         cross(k, 0, 2)
     near(leaves)
+    lists_come(3)
+    index = ((me["x"] * 2 + me["c"]) * 4 + me["y"]) * 4 + me["z"]
+    peers_all = lists.shape[-1]
+    mark = (lax.broadcasted_iota(jnp.int32, (8, peers_all), 1) == index).astype(BF16)
+    table = dot(mark, lists[...].reshape(-1, peers_all).astype(F32).astype(BF16), NT)
+    table_ref[...] = table[:1].astype(jnp.int32)
     for k in colours:
         arrived(k, (2, None, 2))
         for t in (-1, 1):
@@ -346,113 +357,130 @@
         arrival.wait_recv()
     for copy, arrival in crossings:
         copy.wait_send()
-    for copy in started:
+    for copy in started + list_sent:
         copy.wait_send()
     for copy in halo:
         copy.wait_send()
 
 
-def spread(mult, x, near_blocks, near_src, near_count):
-    rows, terms = mult.shape
+def spread(basis, p2m, near_blocks, send_list, send_count, near_src, near_count):
     leaves, slots, panels, _ = near_blocks.shape
-    rhs = x.shape[1]
-    live = lax.broadcasted_iota(jnp.int32, (leaves, slots), 1) < near_count[:, None]
+    rhs = basis.shape[1]
+    terms = p2m.shape[2]
+    rows = leaves * rhs
+    peers = send_list.shape[1]
     tiles = rows // 16
-    cuts = (0, 23 * 16, 43 * 16, tiles * 16)
+    cuts = (0, 22 * 16, 42 * 16, tiles * 16)
     depth = 4
-    hbm = pl.BlockSpec(memory_space=pl.ANY)
+    hbm = pl.BlockSpec(memory_space=pltpu.HBM)
     vmem = pl.BlockSpec(memory_space=pltpu.VMEM)
     smem = pl.BlockSpec(memory_space=pltpu.SMEM)
     dma = pltpu.SemaphoreType.DMA
     return pl.pallas_call(
         functools.partial(spread_kernel, cuts),
-        in_specs=[vmem, hbm, hbm, smem, smem],
-        out_specs=(hbm, vmem),
+        in_specs=[hbm, hbm, hbm, vmem, vmem, smem, smem],
+        out_specs=(hbm, vmem, vmem),
         out_shape=(
             jax.ShapeDtypeStruct((4, 2, 4, 4, rows, terms), BF16),
             jax.ShapeDtypeStruct((rhs, leaves * panels), F32),
+            jax.ShapeDtypeStruct((1, peers * 8), jnp.int32),
         ),
         scratch_shapes=[
             pltpu.VMEM((3 * leaves, rhs, panels), BF16),
             pltpu.VMEM((depth, slots, panels, panels), BF16),
+            pltpu.VMEM((leaves, panels, terms), BF16),
+            pltpu.VMEM((rows, terms), BF16),
+            pltpu.VMEM((8, peers), jnp.int32),
+            pltpu.VMEM((4, 2, 4, 4, 8, peers), jnp.int32),
             dma((3, 12, 4)), dma((3, 12, 4)), dma((3, 16)), dma((3, 16)),
-            dma((2,)), dma((2,)), dma, dma, dma((depth,)),
+            dma((2,)), dma((2,)), dma((4, 3)), dma((4, 3)),
+            dma, dma, dma, dma, dma((depth,)),
         ],
         compiler_params=pltpu.CompilerParams(
-            collective_id=0, has_side_effects=True, vmem_limit_bytes=32 << 20
+            collective_id=0, has_side_effects=True, vmem_limit_bytes=20 << 20
         ),
         name="spread",
-    )(mult, x, near_blocks, near_src.reshape(-1), live.astype(F32).reshape(-1))
+    )(
+        basis, p2m, near_blocks, jnp.swapaxes(send_list, 1, 2), send_count,
+        near_src.T, near_count,
+    )
 
 
 def far_kernel(
-    src_ref, class_ref, table_ref, all_ref, base_ref, p_ref, m2l_ref, basis_ref,
+    src_ref, class_ref, table_ref, all_ref, base_ref, p_hbm, m2l_hbm, basis_ref,
     image_ref, inner_ref,
-    buf, acc, grouped, vbuf, sems, vsem,
+    buf, acc_a, acc_b, grouped, vbuf, p_ref, m2l_ref, sems, vsem,
 ):
     leaves, panels, terms = p_ref.shape
     rhs = base_ref.shape[0]
-    slots = src_ref.shape[0] // leaves
+    slots = src_ref.shape[1]
     classes = m2l_ref.shape[0] // terms
     blocks = basis_ref.shape[0]
     ahead = 4
     group = grouped.shape[0] // rhs
 
-    def entry(i):
-        f = src_ref[i]
-        sender = f // 4
-        leaf = table_ref[sender * 8 + (f - sender * 4)]
-        return sender, leaf
-
     def fetch(leaf):
         def one(e, carry):
-            i = leaf * slots + e
-            sender, at = entry(i)
+            f = src_ref[leaf, e]
+            sender = lax.shift_right_logical(f, 2)
+            at = table_ref[0, sender * 8 + (f & 3)]
             rows = pl.ds(pl.multiple_of(at * rhs, rhs), rhs)
-            pltpu.make_async_copy(all_ref.at[sender, rows], buf.at[i], sems.at[leaf]).start()
+            pltpu.make_async_copy(
+                all_ref.at[sender, rows], buf.at[leaf * slots + e], sems.at[leaf]
+            ).start()
             return carry
 
         lax.fori_loop(0, slots, one, 0, unroll=8)
 
-    whole = pltpu.make_async_copy(basis_ref, vbuf, vsem)
+    loads = [
+        pltpu.make_async_copy(a, b, vsem.at[i])
+        for i, (a, b) in enumerate(((m2l_hbm, m2l_ref), (p_hbm, p_ref), (basis_ref, vbuf)))
+    ]
     for leaf in range(ahead):
         fetch(leaf)
-    whole.start()
+    for load in loads:
+        load.start()
     inner_ref[...] = jnp.zeros_like(inner_ref)
 
     def per_group(g, carry):
-        def per_leaf(j, carry):
-            leaf = g * group + j
-
-            @pl.when(leaf + ahead < leaves)
+        def per_pair(j, carry):
+            first = g * group + j * 2
+
+            @pl.when(first + ahead < leaves)
             def _():
-                fetch(leaf + ahead)
-
-            view = buf.at[pl.ds(leaf * slots, slots)]
-            pltpu.make_async_copy(view, view, sems.at[leaf]).wait()
-            acc[...] = jnp.zeros_like(acc)
+                fetch(first + ahead)
+                fetch(first + ahead + 1)
+
+            for by in range(2):
+                view = buf.at[pl.ds((first + by) * slots, slots)]
+                pltpu.make_async_copy(view, view, sems.at[first + by]).wait()
+            acc_a[...] = jnp.zeros_like(acc_a)
+            acc_b[...] = jnp.zeros_like(acc_b)
 
             def one(e, carry):
-                i = leaf * slots + e
-                f = src_ref[i]
-                sender = f // 4
-                valid = (f - sender * 4) < table_ref[sender * 8 + 4]
-                which = jnp.where(valid, class_ref[i], classes)
-                acc[which] += buf[i].astype(F32)
+                for acc, leaf in ((acc_a, first), (acc_b, first + 1)):
+                    f = src_ref[leaf, e]
+                    sender = lax.shift_right_logical(f, 2)
+                    valid = (f & 3) < table_ref[0, sender * 8 + 4]
+                    which = jnp.where(valid, class_ref[leaf, e], classes)
+                    acc[which] += buf[leaf * slots + e].astype(F32)
                 return carry
 
-            lax.fori_loop(0, slots, one, 0, unroll=8)
-            at = pl.ds(pl.multiple_of(j * rhs, rhs), rhs)
-            for c in range(classes):
-                grouped[at, c * terms : (c + 1) * terms] = acc[c].astype(BF16)
+            lax.fori_loop(0, slots, one, 0, unroll=4)
+            for by, acc in ((0, acc_a), (1, acc_b)):
+                at = pl.ds(pl.multiple_of((j * 2 + by) * rhs, rhs), rhs)
+                for c in range(classes):
+                    grouped[at, c * terms : (c + 1) * terms] = acc[c].astype(BF16)
             return carry
 
-        lax.fori_loop(0, group, per_leaf, 0)
-        local = dot(grouped[...], m2l_ref[...]).astype(BF16)
+        lax.fori_loop(0, group // 2, per_pair, 0)
 
         @pl.when(g == 0)
         def _():
-            whole.wait()
+            for load in loads:
+                load.wait()
+
+        local = dot(grouped[...], m2l_ref[...]).astype(BF16)
 
         for j in range(group):
             leaf = g * group + j
@@ -474,14 +502,14 @@
     blocks, rhs, columns = basis.shape
     slots = far_src.shape[1]
     classes = m2l.shape[0]
-    hbm = pl.BlockSpec(memory_space=pl.ANY)
+    hbm = pl.BlockSpec(memory_space=pltpu.HBM)
     vmem = pl.BlockSpec(memory_space=pltpu.VMEM)
     smem = pl.BlockSpec(memory_space=pltpu.SMEM)
     dma = pltpu.SemaphoreType.DMA
     group = 4
     return pl.pallas_call(
         far_kernel,
-        in_specs=[smem, smem, smem, hbm, vmem, vmem, vmem, hbm],
+        in_specs=[smem, smem, smem, hbm, vmem, hbm, hbm, hbm],
         out_specs=(vmem, vmem),
         out_shape=(
             jax.ShapeDtypeStruct((rhs, columns), F32),
@@ -490,14 +518,17 @@
         scratch_shapes=[
             pltpu.VMEM((leaves * slots, rhs, terms), BF16),
             pltpu.VMEM((classes + 1, rhs, terms), F32),
+            pltpu.VMEM((classes + 1, rhs, terms), F32),
             pltpu.VMEM((group * rhs, classes * terms), BF16),
             pltpu.VMEM((blocks, rhs, columns), BF16),
-            dma((leaves,)), dma,
+            pltpu.VMEM((leaves, panels, terms), BF16),
+            pltpu.VMEM((classes * terms, terms), BF16),
+            dma((leaves,)), dma((3,)),
         ],
-        compiler_params=pltpu.CompilerParams(vmem_limit_bytes=40 << 20),
+        compiler_params=pltpu.CompilerParams(vmem_limit_bytes=28 << 20),
         name="far_field",
     )(
-        far_src.reshape(-1), far_class.reshape(-1), table, everyone, base, p2m,
+        far_src, far_class, table, everyone, base, p2m,
         m2l.reshape(classes * terms, terms), basis,
     )
 
@@ -636,7 +667,7 @@
 def finish(inner, image, basis, total_rows):
     blocks, rhs, columns = basis.shape
     wide = blocks * rhs
-    hbm = pl.BlockSpec(memory_space=pl.ANY)
+    hbm = pl.BlockSpec(memory_space=pltpu.HBM)
     vmem = pl.BlockSpec(memory_space=pltpu.VMEM)
     dma = pltpu.SemaphoreType.DMA
     return pl.pallas_call(
@@ -661,7 +692,7 @@
             dma((2, 8)), dma((2, 8)), dma((2, 16)), dma((2, 16)), dma((2, 8)), dma((2, 8)), dma,
         ],
         compiler_params=pltpu.CompilerParams(
-            collective_id=1, has_side_effects=True, vmem_limit_bytes=32 << 20
+            collective_id=1, has_side_effects=True, vmem_limit_bytes=20 << 20
         ),
         name="finish",
     )(inner, image, basis)
@@ -673,14 +704,10 @@
     blocks, rhs, columns = basis.shape
     leaves, panels, terms = p2m.shape
     peers = lax.axis_size(ALL)
-    slots = send_list.shape[2]
-    mult, x = multipoles(basis, p2m, send_list, send_count)
-    everyone, base = spread(mult, x, near_blocks, near_src, near_count)
-    everyone = everyone.reshape(peers, *mult.shape)
-    rows = leaves * rhs
-    lists = lax.slice(everyone, (0, rows, 0), (peers, rows + 8, terms))
-    me = lax.axis_index(ALL)
-    table = lax.dynamic_slice_in_dim(lists, me, 1, axis=2).astype(jnp.int32).reshape(-1)
+    everyone, base, table = spread(
+        basis, p2m, near_blocks, send_list, send_count, near_src, near_count
+    )
+    everyone = everyone.reshape(peers, leaves * rhs, terms)
     image, inner = far_field(far_src, far_class, table, everyone, base, p2m, m2l, basis)
     new, proj, upper = finish(inner, image, basis, columns * peers)
     factor = upper[:, :rhs].T

time: 163 us -> 152 us (0.933)
  Pallas kernels: 142 us -> 137 us
  local copies, waits for them, and re-layouts: 17.2 us -> 14.1 us
  other arithmetic: 3.06 us -> 0 us
    pallas_call x3 -> x2, Pallas kernels: 106 us -> 103 us  [the longest x1 89.6 us: spread(): pl.pallas_call(functools.partial(spread_kernel, cuts), in_specs=[hbm, hbm...]
    reshape x1 -> x0, other arithmetic: 2.33 us -> none  [shards(): lax.dynamic_slice_in_dim(lists, me, 1, axis=2).astype(jnp.int32).reshape(-1)]
    reshape x4 -> x0, local copies, waits for them, and re-layouts: 1.84 us -> none  [the longest x1 0.89 us: far_field(): far_src.reshape(-1)]
    unnamed x17 -> x27, local copies, waits for them, and re-layouts: 14.3 us -> 14.1 us
where the time goes in v2:
time: 152 us
  Pallas kernels  137 us (90%)
  local copies, waits for them, and re-layouts  14.1 us (9%)
    pallas_call x1, Pallas kernels, spread(): pl.pallas_call(functools.partial(spread_kernel, cuts), in_specs=[hbm, hbm...  89.6 us
    pallas_call x1, Pallas kernels, finish(): pl.pallas_call(functools.partial(finish_kernel, total_rows), in_specs=[vm...  34.4 us
    unnamed x27, local copies, waits for them, and re-layouts  14.1 us
    pallas_call x1, Pallas kernels, far_field(): pl.pallas_call(far_kernel, in_specs=[smem, smem, smem, hbm, vmem, hbm, hb...  13.2 us

profile of v2, /device:TPU:1, one launch (start us, length us, event | category | flops | bytes accessed | tf_op | source)
XLA Modules:
  0.0 152.1 jit_solution(6393090653753679188)
XLA Ops:
  0.6 0.0 copy-start
  0.6 2.2 %copy-done = bf16[8,64,4096]{2,1,0:T(8,128)(2,1)S(1)} copy-done((bf16[8,64,4096]{2,1,0:T(8,128)(2,1)S(1)}, bf16[8,64,4096]{2,1,0:T(8,128)(2,1)}, u32[]{:S(2)}) %copy-start) | copy-done | bytes 4194328
  2.8 0.0 copy-start.2
  2.8 5.8 %copy-done.2 = bf16[16,8,256,256]{3,2,1,0:T(8,128)(2,1)S(1)} copy-done((bf16[16,8,256,256]{3,2,1,0:T(8,128)(2,1)S(1)}, bf16[16,8,256,256]{3,2,1,0:T(8,128)(2,1)}, u32[]{:S(2)}) %copy-start.2) | copy-done | bytes 16777240
  8.6 0.0 copy-start.3
  8.6 1.2 copy-done.3
  9.8 0.0 copy-start.8
  9.8 0.7 copy-done.8
  10.5 0.0 copy-start.9
  10.5 0.7 copy-done.9
  11.2 0.7 copy-done.10
  11.8 0.7 copy-done.11
  12.5 0.0 copy-start.7
  12.5 89.6 %spread.1 = (bf16[4,2,4,4,1024,128]{5,4,3,2,1,0:T(8,128)(2,1)}, f32[64,4096]{1,0:T(8,128)S(1)}, s32[1,1024]{1,0:T(1,128)S(1)}) custom-call(bf16[8,64,4096]{2,1,0:T(8,128)(2,1)S(1)} %copy-done, bf16[16,256,128]{2,1,0:T(8,128)(2,1)S(1)} %copy-done.3, bf16[16,8,256,256]{3,2,1,0:T(8,128)(2,1)S(1)} %copy-done.2, s32[1,4,128]{2,1,0:T(4,128)S(1)} %bitcast.10, ...), custom_call_target="tpu_custom_call" | custom-call | tf_op jit(solution)/shard_map/spread/pallas_call | solution.py:379
  102.2 0.0 copy-done.1
  102.2 0.0 copy-done.4
  102.2 0.0 copy-done.5
  102.2 0.0 copy-done.6
  102.2 0.0 copy-done.7
  102.2 13.2 %far_field.1 = (f32[64,4096]{1,0:T(8,128)S(1)}, f32[64,512]{1,0:T(8,128)S(1)}) custom-call(s32[16,32]{1,0:T(8,128)S(1)} %copy-done.6, s32[16,32]{1,0:T(8,128)S(1)} %copy-done.7, s32[1,1024]{1,0:T(1,128)S(1)} %get-tuple-element.11.table_ref, bf16[128,1024,128]{2,1,0:T(8,128)(2,1)} %bitcast.11, f32[64,4096]{1,0:T(8,128)S(1)} %get-tuple-element.13.base_ref, ...), custom_call_target="tpu_custom_call" | custom-call | tf_op jit(solution)/shard_map/far_field/pallas_call | solution.py:510
  115.5 34.4 %finish.1 = (bf16[64,4096]{1,0:T(8,128)(2,1)S(1)}, f32[512,64]{1,0:T(8,128)S(1)}, f32[64,128]{1,0:T(8,128)S(1)}) custom-call(f32[64,512]{1,0:T(8,128)S(1)} %get-tuple-element.14.inner_ref, f32[64,4096]{1,0:T(8,128)S(1)} %get-tuple-element.15.image_ref, bf16[8,64,4096]{2,1,0:T(8,128)(2,1)S(1)} %copy-done.1), custom_call_target="tpu_custom_call" | custom-call | tf_op jit(solution)/shard_map/finish/pallas_call | solution.py:673
  149.9 0.7 copy.13
  150.6 0.8 copy.16
  151.4 0.7 copy.17
  (7 shorter events, 0.0 us)
Async XLA Ops:
  0.6 2.2 %copy-start = (bf16[8,64,4096]{2,1,0:T(8,128)(2,1)S(1)}, bf16[8,64,4096]{2,1,0:T(8,128)(2,1)}, u32[]{:S(2)}) copy-start(bf16[8,64,4096]{2,1,0:T(8,128)(2,1)} %basis_ref.5) | copy-start | bytes 12582916
  2.8 5.8 %copy-start.2 = (bf16[16,8,256,256]{3,2,1,0:T(8,128)(2,1)S(1)}, bf16[16,8,256,256]{3,2,1,0:T(8,128)(2,1)}, u32[]{:S(2)}) copy-start(bf16[16,8,256,256]{3,2,1,0:T(8,128)(2,1)} %near_blocks_ref.1) | copy-start | bytes 50331652
  8.6 1.2 copy-start.3
  9.8 0.7 copy-start.8
  10.5 0.7 copy-start.9
  11.2 0.7 copy-start.10
  11.8 0.7 copy-start.11
  12.5 89.7 %copy-start.1 = (bf16[8,64,4096]{2,1,0:T(8,128)(2,1)S(1)}, bf16[8,64,4096]{2,1,0:T(8,128)(2,1)}, u32[]{:S(2)}) copy-start(bf16[8,64,4096]{2,1,0:T(8,128)(2,1)} %basis_ref.5) | copy-start | bytes 12582916
  12.5 89.7 %copy-start.4 = (bf16[16,256,128]{2,1,0:T(8,128)(2,1)S(1)}, bf16[16,256,128]{2,1,0:T(8,128)(2,1)}, u32[]{:S(2)}) copy-start(bf16[16,256,128]{2,1,0:T(8,128)(2,1)} %p_hbm.1) | copy-start | bytes 3145732
  12.5 89.7 %copy-start.5 = (bf16[16,128,128]{2,1,0:T(8,128)(2,1)S(1)}, bf16[16,128,128]{2,1,0:T(8,128)(2,1)}, u32[]{:S(2)}) copy-start(bf16[16,128,128]{2,1,0:T(8,128)(2,1)} %param.15) | copy-start | bytes 1572868
  12.5 89.7 %copy-start.6 = (s32[16,32]{1,0:T(8,128)S(1)}, s32[16,32]{1,0:T(8,128)}, u32[]{:S(2)}) copy-start(s32[16,32]{1,0:T(8,128)} %src_ref.1) | copy-start | bytes 6148
  12.5 89.7 %copy-start.7 = (s32[16,32]{1,0:T(8,128)S(1)}, s32[16,32]{1,0:T(8,128)}, u32[]{:S(2)}) copy-start(s32[16,32]{1,0:T(8,128)} %class_ref.1) | copy-start | bytes 6148

commit v3 on v2

--- a/solution.py
+++ b/solution.py
@@ -74,6 +74,19 @@
     stage[:slots_out, :] = list_ref[0]
     stage[slots_out : slots_out + 1, :] = count_ref[...]
     pltpu.make_async_copy(mine, mine, x_sem).wait()
+    pl.semaphore_wait(barrier, len(peers))
+    halo = []
+    for i, (target, slot) in enumerate(((after, 0), (before, 2))):
+        copy = pltpu.make_async_remote_copy(
+            src_ref=mine,
+            dst_ref=xbuf.at[pl.ds(slot * leaves, leaves)],
+            send_sem=halo_send.at[i],
+            recv_sem=halo_recv.at[i],
+            device_id=target,
+            device_id_type=MESH,
+        )
+        copy.start()
+        halo.append(copy)
     load_p.wait()
 
     def multipole(leaf, carry):
@@ -88,7 +101,6 @@
     my_list = lists.at[me["x"], me["c"], me["y"], me["z"]]
     keep_list = pltpu.make_async_copy(stage, my_list, stage_sem)
     keep_list.start()
-    pl.semaphore_wait(barrier, len(peers))
 
     def place(where, rows, core):
         index = []
@@ -269,19 +281,6 @@
     for unit in (units[0], (1, 0, None), (2, 0, 0)):
         for k in colours:
             send(k, unit)
-    halo = []
-    for i, (target, slot) in enumerate(((after, 0), (before, 2))):
-        copy = pltpu.make_async_remote_copy(
-            src_ref=mine,
-            dst_ref=xbuf.at[pl.ds(slot * leaves, leaves)],
-            send_sem=halo_send.at[i],
-            recv_sem=halo_recv.at[i],
-            device_id=target,
-            device_id_type=MESH,
-        )
-        copy.start()
-        halo.append(copy)
-
     for k in colours:
         arrived(k, units[0])
         for r in (-1, 1):
@@ -397,7 +396,7 @@
             dma, dma, dma, dma, dma((depth,)),
         ],
         compiler_params=pltpu.CompilerParams(
-            collective_id=0, has_side_effects=True, vmem_limit_bytes=20 << 20
+            collective_id=0, has_side_effects=True, vmem_limit_bytes=LIMIT
         ),
         name="spread",
     )(
@@ -525,7 +524,7 @@
             pltpu.VMEM((classes * terms, terms), BF16),
             dma((leaves,)), dma((3,)),
         ],
-        compiler_params=pltpu.CompilerParams(vmem_limit_bytes=28 << 20),
+        compiler_params=pltpu.CompilerParams(vmem_limit_bytes=LIMIT),
         name="far_field",
     )(
         far_src, far_class, table, everyone, base, p2m,
@@ -536,32 +535,35 @@
 def finish_kernel(
     total_rows, inner_ref, image_ref, basis_ref,
     next_ref, proj_ref, factor_ref,
-    vbuf, gram_in, one_in, two_in, stack, piece, whole, gone, two_gone,
-    s1, r1, s2, r2, s3, r3, vsem,
+    vbuf, image, gram_in, one_in, two_in, stack, piece, whole, gone, narrow, two_gone,
+    s1, r1, s2, r2, s3, r3, vsem, isem,
 ):
     me = {name: lax.axis_index(name) for name in ALL}
     column = me["x"] * 2 + me["c"]
-    segment = me["y"] * 4 + me["z"]
-    gx, bulk = 8, 16
+    gx = 8
     rhs, columns = image_ref.shape
     blocks = basis_ref.shape[0]
     load = pltpu.make_async_copy(basis_ref, vbuf, vsem)
     load.start()
+    load_image = pltpu.make_async_copy(image_ref, image, isem)
+    load_image.start()
 
     def col_peer(by):
         c = lax.rem(column + by, gx)
         return c, {"x": c // 2, "c": lax.rem(c, 2)}
 
-    def seg_peer(by):
-        s = lax.rem(segment + by, bulk)
-        return s, {"y": s // 4, "z": lax.rem(s, 4)}
+    def line_peer(axis, by):
+        c = lax.rem(me[axis] + by, 4)
+        return c, {axis: c}
 
     barrier = pltpu.get_barrier_semaphore()
     for by in range(1, gx):
         pl.semaphore_signal(barrier, inc=1, device_id=col_peer(by)[1], device_id_type=MESH)
-    for by in range(1, bulk):
-        pl.semaphore_signal(barrier, inc=1, device_id=seg_peer(by)[1], device_id_type=MESH)
-    pl.semaphore_wait(barrier, gx + bulk - 2)
+    for axis in ("y", "z"):
+        for by in range(1, 4):
+            peer = line_peer(axis, by)[1]
+            pl.semaphore_signal(barrier, inc=1, device_id=peer, device_id_type=MESH)
+    pl.semaphore_wait(barrier, gx - 1 + 6)
 
     def remote(src, dst, send, recv, peer):
         return pltpu.make_async_remote_copy(
@@ -583,19 +585,25 @@
         for by in range(1, gx):
             remote(arrivals.at[by], arrivals.at[by], s1.at[n, by], r1.at[n, by], col_peer(1)[1]).wait_recv()
             total = total + arrivals[by]
-        mine[...] = total
-        for by in range(1, bulk):
-            s, peer = seg_peer(by)
-            copy = remote(mine, parts.at[segment], s2.at[n, by], r2.at[n, bulk - by], peer)
-            copy.start()
-            sent.append(copy)
-        parts[segment] = total
-        for by in range(1, bulk):
-            s, peer = seg_peer(by)
-            remote(mine, parts.at[s], s2.at[n, by], r2.at[n, by], peer).wait_recv()
-        total = parts[0]
-        for s in range(1, bulk):
-            total = total + parts[s]
+        for n_axis, axis in enumerate(("y", "z")):
+            slot = mine.at[n_axis]
+            slot[...] = total
+            for by in range(1, 4):
+                i = n_axis * 4 + by
+                copy = remote(
+                    slot, parts.at[n_axis * 4 + me[axis]],
+                    s2.at[n, i], r2.at[n, n_axis * 4 + 4 - by], line_peer(axis, by)[1],
+                )
+                copy.start()
+                sent.append(copy)
+            parts[n_axis * 4 + me[axis]] = total
+            for by in range(1, 4):
+                c, peer = line_peer(axis, by)
+                i = n_axis * 4 + by
+                remote(slot, parts.at[n_axis * 4 + c], s2.at[n, i], r2.at[n, i], peer).wait_recv()
+            total = parts[n_axis * 4]
+            for c in range(1, 4):
+                total = total + parts[n_axis * 4 + c]
         result[own, :] = total
         for by in range(1, gx):
             c, peer = col_peer(by)
@@ -612,6 +620,7 @@
     scale = 1.0 / total_rows
     all_reduce(0, inner_ref, one_in, piece, two_in, whole)
     load.wait()
+    load_image.wait()
     proj = whole[...] * scale
     coef = jnp.concatenate(halves(proj), axis=0)
     step = 512
@@ -619,14 +628,14 @@
     for i in range(0, columns, step):
         v = vbuf[:, :, i : i + step].reshape(blocks * rhs, step)
         out = dot(coef, v)
-        resid = image_ref[:, i : i + step] - (out[:rhs] + out[rhs:])
+        resid = image[:, i : i + step] - (out[:rhs] + out[rhs:])
         both = jnp.concatenate(halves(resid), axis=0)
         stack[:, i : i + step] = both
         gram = gram + dot(both, both, NT)
     gram_in[...] = gram[:rhs] + gram[rhs:]
     for i in range(0, blocks * rhs, 2 * rhs):
         proj_ref[i : i + 2 * rhs, :] = proj[:, i : i + 2 * rhs].T
-    all_reduce(1, gram_in, gone, piece.at[:, : 2 * rhs], two_gone, factor_ref)
+    all_reduce(1, gram_in, gone, narrow, two_gone, factor_ref)
     folded = factor_ref[...] * scale
     folded = folded + pltpu.roll(folded, rhs, 1)
     lane = lax.broadcasted_iota(jnp.int32, (rhs, 2 * rhs), 1)
@@ -672,7 +681,7 @@
     dma = pltpu.SemaphoreType.DMA
     return pl.pallas_call(
         functools.partial(finish_kernel, total_rows),
-        in_specs=[vmem, vmem, hbm],
+        in_specs=[vmem, hbm, hbm],
         out_specs=(vmem, vmem, vmem),
         out_shape=(
             jax.ShapeDtypeStruct((rhs, columns), BF16),
@@ -681,18 +690,20 @@
         ),
         scratch_shapes=[
             pltpu.VMEM((blocks, rhs, columns), BF16),
+            pltpu.VMEM((rhs, columns), F32),
             pltpu.VMEM((rhs, 2 * rhs), F32),
             pltpu.VMEM((8, 8, wide), F32),
-            pltpu.VMEM((16, 8, wide), F32),
+            pltpu.VMEM((8, 8, wide), F32),
             pltpu.VMEM((2 * rhs, columns), BF16),
-            pltpu.VMEM((8, wide), F32),
+            pltpu.VMEM((2, 8, wide), F32),
             pltpu.VMEM((rhs, wide), F32),
             pltpu.VMEM((8, 8, 2 * rhs), F32),
-            pltpu.VMEM((16, 8, 2 * rhs), F32),
-            dma((2, 8)), dma((2, 8)), dma((2, 16)), dma((2, 16)), dma((2, 8)), dma((2, 8)), dma,
+            pltpu.VMEM((2, 8, 2 * rhs), F32),
+            pltpu.VMEM((8, 8, 2 * rhs), F32),
+            dma((2, 8)), dma((2, 8)), dma((2, 8)), dma((2, 8)), dma((2, 8)), dma((2, 8)), dma, dma,
         ],
         compiler_params=pltpu.CompilerParams(
-            collective_id=1, has_side_effects=True, vmem_limit_bytes=20 << 20
+            collective_id=1, has_side_effects=True, vmem_limit_bytes=LIMIT
         ),
         name="finish",
     )(inner, image, basis)

time: 152 us -> 153 us (level)
  Pallas kernels: 137 us -> 147 us
  local copies, waits for them, and re-layouts: 14.1 us -> 5 us
    unnamed x27 -> x3, local copies, waits for them, and re-layouts: 14.1 us -> 4.24 us
    pallas_call x1, Pallas kernels: 89.6 us -> 94.9 us  [spread(): pl.pallas_call(functools.partial(spread_kernel, cuts), in_specs=[hbm, hbm...]
    pallas_call x1, Pallas kernels: 34.4 us -> 36.7 us  [finish(): pl.pallas_call(functools.partial(finish_kernel, total_rows), in_specs=[vm...]
    pallas_call x1, Pallas kernels: 13.2 us -> 15.1 us  [far_field(): pl.pallas_call(far_kernel, in_specs=[smem, smem, smem, hbm, vmem, hbm, hb...]
where the time goes in v3:
time: 153 us; the launch traced here: 152 us
  Pallas kernels  147 us (96%)
  local copies, waits for them, and re-layouts  5 us (3%)
    pallas_call x1, Pallas kernels, spread(): pl.pallas_call(functools.partial(spread_kernel, cuts), in_specs=[hbm, hbm...  94.9 us
    pallas_call x1, Pallas kernels, finish(): pl.pallas_call(functools.partial(finish_kernel, total_rows), in_specs=[vm...  36.7 us
    pallas_call x1, Pallas kernels, far_field(): pl.pallas_call(far_kernel, in_specs=[smem, smem, smem, hbm, vmem, hbm, hb...  15.1 us
    unnamed x3, local copies, waits for them, and re-layouts  4.24 us

profile of v3, /device:TPU:1, one launch (start us, length us, event | category | flops | bytes accessed | tf_op | source)
XLA Modules:
  0.0 152.4 jit_solution(3054965858868391048)
XLA Ops:
  0.6 94.9 %spread.1 = (bf16[4,2,4,4,1024,128]{5,4,3,2,1,0:T(8,128)(2,1)}, f32[64,4096]{1,0:T(8,128)}, s32[1,1024]{1,0:T(1,128)}) custom-call(bf16[8,64,4096]{2,1,0:T(8,128)(2,1)} %basis_ref.5, bf16[16,256,128]{2,1,0:T(8,128)(2,1)} %p_hbm.1, bf16[16,8,256,256]{3,2,1,0:T(8,128)(2,1)} %near_blocks_ref.1, s32[1,4,128]{2,1,0:T(4,128)} %bitcast.11, s32[1,128]{1,0:T(1,128)} %count_ref.1, ...), custom_call_target="tpu_custom_call" | custom-call | tf_op jit(solution)/shard_map/spread/pallas_call | solution.py:378
  95.6 15.1 %far_field.1 = (f32[64,4096]{1,0:T(8,128)}, f32[64,512]{1,0:T(8,128)}) custom-call(s32[16,32]{1,0:T(8,128)} %src_ref.1, s32[16,32]{1,0:T(8,128)} %class_ref.1, s32[1,1024]{1,0:T(1,128)} %get-tuple-element.11.table_ref, bf16[128,1024,128]{2,1,0:T(8,128)(2,1)} %bitcast.7, f32[64,4096]{1,0:T(8,128)} %get-tuple-element.13.base_ref, bf16[16,256,128]{2,1,0:T(8,128)(2,1)} %p_hbm.1, ...), custom_call_target="tpu_custom_call" | custom-call | tf_op jit(solution)/shard_map/far_field/pallas_call | solution.py:509
  110.7 36.7 %finish.1 = (bf16[64,4096]{1,0:T(8,128)(2,1)}, f32[512,64]{1,0:T(8,128)}, f32[64,128]{1,0:T(8,128)}) custom-call(f32[64,512]{1,0:T(8,128)} %get-tuple-element.14.inner_ref, f32[64,4096]{1,0:T(8,128)} %get-tuple-element.15.image_ref, bf16[8,64,4096]{2,1,0:T(8,128)(2,1)} %basis_ref.5), custom_call_target="tpu_custom_call" | custom-call | tf_op jit(solution)/shard_map/finish/pallas_call | solution.py:682
  147.4 0.8 slice_bitcast_fusion
  148.2 0.7 copy.13
  148.9 1.9 %copy.16 = bf16[64,4096]{1,0:T(8,128)(2,1)} copy(bf16[64,4096]{1,0:T(8,128)(2,1)} %get-tuple-element.25) | data formatting | bytes 1048576
  150.8 1.7 %copy.17 = f32[8,64,64]{2,1,0:T(8,128)} copy(f32[8,64,64]{2,1,0:T(8,128)} %bitcast.9) | data formatting | bytes 262144

commit v4 on v3

v4 whole, which is shorter than its diff:
```python
import functools

import jax
import jax.numpy as jnp
from jax import lax
from jax.experimental import pallas as pl
from jax.experimental.pallas import tpu as pltpu
from jax.sharding import Mesh
from jax.sharding import PartitionSpec as P

ALL = ("x", "c", "y", "z")
ORDERS = (("x", "y", "z"), ("y", "z", "x"), ("z", "x", "y"))
MESH = pl.DeviceIdType.MESH
F32, BF16 = jnp.float32, jnp.bfloat16
LIMIT = 67043328
NT = (((1,), (1,)), ((), ()))
TN = (((0,), (0,)), ((), ()))


def dot(a, b, dims=(((1,), (0,)), ((), ()))):
    return lax.dot_general(a, b, dims, preferred_element_type=F32)


def halves(values):
    upper = values.astype(BF16)
    return upper, (values - upper.astype(F32)).astype(BF16)


def step_kernel(
    cuts, total_rows, basis_ref, p_ref, near_blocks_ref, m2l_ref, list_ref, count_ref,
    src_ref, near_count_ref, far_ref, class_ref,
    next_ref, proj_ref, factor_ref,
    all_ref, xbuf, nbuf, pbuf, mbuf, stage, lists, base_ref, vbuf, mats, table_ref, table,
    inner_ref, gram_in, one_in, two_in, stack, piece, whole, gone, narrow, two_gone, gram_out,
    s1, r1, s2, r2, s3, r3, v_sem, m_sem, t_sem,
    send_sem, recv_sem, sib_send, sib_recv, halo_send, halo_recv, list_send, list_recv,
    own_sem, x_sem, p_sem, stage_sem, nsem,
):
    me = {name: lax.axis_index(name) for name in ALL}
    leaves = near_blocks_ref.shape[0]
    slots = near_blocks_ref.shape[1]
    panels = near_blocks_ref.shape[2]
    depth = nbuf.shape[0]
    column = me["x"] * 2 + me["c"]

    def at(axis, by):
        return lax.rem(me[axis] + (by + 4), 4)

    def near_copy(leaf, slot):
        return pltpu.make_async_copy(near_blocks_ref.at[leaf], nbuf.at[slot], nsem.at[slot])

    blocks, rhs = basis_ref.shape[:2]
    mine = xbuf.at[pl.ds(leaves, leaves)]
    for leaf in range(leaves):
        pltpu.make_async_copy(
            basis_ref.at[blocks - 1, :, pl.ds(leaf * panels, panels)], mine.at[leaf], x_sem
        ).start()
    load_p = pltpu.make_async_copy(p_ref, pbuf, p_sem)
    load_p.start()
    load_v = pltpu.make_async_copy(basis_ref, vbuf, v_sem)
    load_v.start()
    classes, terms = m2l_ref.shape[:2]
    load_m = pltpu.make_async_copy(m2l_ref, mats.at[pl.ds(0, classes)], m_sem)
    load_m.start()
    mats[classes] = jnp.zeros((terms, terms), BF16)
    for leaf in range(depth):
        near_copy(leaf, leaf).start()

    other = {"c": 1 - me["c"]}
    barrier = pltpu.get_barrier_semaphore()
    gx = 8

    def col_peer(by):
        c = lax.rem(column + by, gx)
        return c, {"x": c // 2, "c": lax.rem(c, 2)}

    def line_peer(axis, by):
        c = lax.rem(me[axis] + by, 4)
        return c, {axis: c}

    after, before = col_peer(1)[1], col_peer(gx - 1)[1]
    peers = [col_peer(by)[1] for by in range(1, gx)]
    peers += [line_peer(axis, by)[1] for axis in ("y", "z") for by in range(1, 4)]
    for peer in peers:
        pl.semaphore_signal(barrier, inc=1, device_id=peer, device_id_type=MESH)
    slots_out = list_ref.shape[1]
    stage[...] = jnp.zeros_like(stage)
    stage[:slots_out, :] = list_ref[0]
    stage[slots_out : slots_out + 1, :] = count_ref[...]
    def list_region(stage_index):
        index = [me["x"], me["c"], me["y"], me["z"]]
        for place_of in ((), (0,), (0, 2), (0, 2, 3))[stage_index]:
            index[place_of] = slice(None)
        return lists.at[tuple(index)]

    def list_copies(i):
        if i == 3:
            targets = [other]
        else:
            axis = ("x", "y", "z")[i]
            targets = [{axis: at(axis, by)} for by in (1, 2, 3)]
        region = list_region(i)
        out = []
        for t, target in enumerate(targets):
            out.append(
                pltpu.make_async_remote_copy(
                    src_ref=region, dst_ref=region,
                    send_sem=list_send.at[i, t], recv_sem=list_recv.at[i, t],
                    device_id=target, device_id_type=MESH,
                )
            )
        return out

    list_sent = []

    def lists_go(i):
        for copy in list_copies(i):
            copy.start()
            list_sent.append(copy)

    def lists_come(i):
        for copy in list_copies(i):
            copy.wait_recv()

    my_list = lists.at[me["x"], me["c"], me["y"], me["z"]]
    keep_list = pltpu.make_async_copy(stage, my_list, stage_sem)
    keep_list.start()
    pltpu.make_async_copy(mine, mine, x_sem).wait()
    load_p.wait()
    keep_list.wait()
    pl.semaphore_wait(barrier, len(peers))
    lists_go(0)

    def multipole(leaf, carry):
        block = dot(xbuf[leaves + leaf], pbuf[leaf]).astype(BF16)
        mbuf[2 * leaf] = block[: rhs // 2]
        mbuf[2 * leaf + 1] = block[rhs // 2 :]
        return carry

    lax.fori_loop(0, leaves, multipole, 0, unroll=4)
    here = all_ref.at[me["x"], me["c"], me["y"], me["z"]]
    keep = pltpu.make_async_copy(mbuf, here, own_sem)
    keep.start()

    def place(where, rows, core):
        index = []
        for name in ALL:
            if name == "c":
                index.append(core)
            elif name in where:
                index.append(where[name])
            else:
                index.append(slice(None))
        return all_ref.at[tuple(index) + (pl.ds(rows[0], rows[1] - rows[0]),)]

    units = [(0, None, None)]
    units += [(1, r, None) for r in (0, -1, 1, 2)]
    units += [(2, r, 0) for r in (0, -1, 1, 2)]
    units += [(2, None, r) for r in (-1, 1, 2)]
    number = {u: i for i, u in enumerate(units)}
    started = []

    def where_of(colour, unit, by):
        axes = ORDERS[colour]
        phase, first, second = unit
        where = {}
        if phase == 0:
            where = {axes[0]: by, axes[1]: 0, axes[2]: 0}
        elif phase == 1:
            where = {axes[0]: first, axes[1]: by, axes[2]: 0}
        else:
            where = {axes[1]: second, axes[2]: by}
            if first is not None:
                where[axes[0]] = first
        return where

    def rows_of(colour, part):
        low, high = cuts[colour], cuts[colour + 1]
        middle = low + (high - low) // 2
        return {"all": (low, high), "lower": (low, middle), "upper": (middle, high)}[part]

    def remote(colour, unit, kind):
        axis = ORDERS[colour][unit[0]]
        by, to, part = ((0, 1, "all"), (0, -1, "all"), (-1, 1, "lower"), (1, -1, "upper"))[kind]
        offsets = where_of(colour, unit, by)
        where = {name: at(name, v) for name, v in offsets.items()}
        rows = rows_of(colour, part)
        dst = place(where, rows, me["c"])
        i = number[unit]
        return pltpu.make_async_remote_copy(
            src_ref=dst,
            dst_ref=dst,
            send_sem=send_sem.at[colour, i, kind],
            recv_sem=recv_sem.at[colour, i, kind],
            device_id={axis: at(axis, to)},
            device_id_type=MESH,
        )

    def send(colour, unit):
        for kind in (0, 1):
            copy = remote(colour, unit, kind)
            copy.start()
            started.append(copy)

    def arrived(colour, unit):
        for kind in (0, 1):
            remote(colour, unit, kind).wait_recv()
        for kind in (2, 3):
            copy = remote(colour, unit, kind)
            copy.start()
            started.append(copy)

    def arrived_far(colour, unit):
        for kind in (2, 3):
            remote(colour, unit, kind).wait_recv()

    crossings = []

    def cross(colour, second, third):
        axes = ORDERS[colour]
        where = {axes[1]: at(axes[1], second), axes[2]: at(axes[2], third)}
        ref = place(where, rows_of(colour, "all"), me["c"])
        i = ((0, -1, 1, 2).index(second)) * 4 + (0, -1, 1, 2).index(third)
        copy = pltpu.make_async_remote_copy(
            src_ref=ref,
            dst_ref=ref,
            send_sem=sib_send.at[colour, i],
            recv_sem=sib_recv.at[colour, i],
            device_id=other,
            device_id_type=MESH,
        )
        copy.start()
        other_ref = place(where, rows_of(colour, "all"), other["c"])
        arrival = pltpu.make_async_remote_copy(
            src_ref=other_ref,
            dst_ref=other_ref,
            send_sem=sib_send.at[colour, i],
            recv_sem=sib_recv.at[colour, i],
            device_id=other,
            device_id_type=MESH,
        )
        crossings.append((copy, arrival))

    done_leaves = [0]

    def near(count):
        first = done_leaves[0]
        last = min(leaves, first + count)
        done_leaves[0] = last
        if last == first:
            return
        if first == 0:
            for copy in halo:
                copy.wait_recv()

            @pl.when(column == 0)
            def _():
                xbuf[:leaves] = jnp.zeros((leaves,) + xbuf.shape[1:], BF16)

            @pl.when(column == gx - 1)
            def _():
                xbuf[2 * leaves :] = jnp.zeros((leaves,) + xbuf.shape[1:], BF16)

        def body(leaf, carry):
            slot = lax.rem(leaf, depth)
            near_copy(leaf, slot).wait()
            lanes = pl.ds(pl.multiple_of(leaf * panels, panels), panels)
            total = xbuf[leaves + leaf].astype(F32)
            for k in range(slots):
                live = lax.min(lax.max(near_count_ref[leaf] - k, 0), 1).astype(F32)
                total = total + live * dot(xbuf[src_ref[k, leaf]], nbuf[slot, k], NT)
            base_ref[:, lanes] = total

            @pl.when(leaf + depth < leaves)
            def _():
                near_copy(leaf + depth, slot).start()

            return carry

        lax.fori_loop(first, last, body, 0)

    colours = range(3)
    keep.wait()
    for k in colours:
        send(k, units[0])
    lists_come(0)
    lists_go(1)
    for k in colours:
        send(k, (1, 0, None))
    for k in colours:
        arrived(k, units[0])
        for r in (-1, 1):
            send(k, (1, r, None))
    lists_come(1)
    lists_go(2)
    for k in colours:
        arrived_far(k, units[0])
        send(k, (1, 2, None))
    for k in colours:
        send(k, (2, 0, 0))
    for k in colours:
        arrived(k, (1, 0, None))
        for r in (-1, 1, 2):
            send(k, (2, r, 0))
    for k in colours:
        cross(k, 0, 0)
    for r in (-1, 1, 2):
        for k in colours:
            arrived(k, (1, r, None))
    for k in colours:
        arrived(k, (2, 0, 0))
    for r in (-1, 1):
        for k in colours:
            send(k, (2, None, r))
    halo = []
    for i, (target, slot) in enumerate(((after, 0), (before, 2))):
        copy = pltpu.make_async_remote_copy(
            src_ref=mine,
            dst_ref=xbuf.at[pl.ds(slot * leaves, leaves)],
            send_sem=halo_send.at[i],
            recv_sem=halo_recv.at[i],
            device_id=target,
            device_id_type=MESH,
        )
        copy.start()
        halo.append(copy)
    for r in (0, -1, 1, 2):
        for k in colours:
            arrived_far(k, (1, r, None))
    for k in colours:
        send(k, (2, None, 2))
    for r in (-1, 1, 2):
        for k in colours:
            cross(k, r, 0)
    lists_come(2)
    lists_go(3)
    for r in (-1, 1, 2):
        for k in colours:
            arrived(k, (2, r, 0))
    for k in colours:
        for t in (-1, 1):
            cross(k, 0, t)
    for r in (-1, 1):
        for k in colours:
            arrived(k, (2, None, r))
            for t in (-1, 1):
                cross(k, r, t)
            if r == 1:
                near(2)
    for r in (0, -1, 1, 2):
        for k in colours:
            arrived_far(k, (2, r, 0))
        near(2)
    for k in colours:
        cross(k, 0, 2)
    near(leaves)
    lists_come(3)
    index = ((me["x"] * 2 + me["c"]) * 4 + me["y"]) * 4 + me["z"]
    peers_all = lists.shape[-1]
    mark = (lax.broadcasted_iota(jnp.int32, (8, peers_all), 1) == index).astype(BF16)
    picked = dot(mark, lists[...].reshape(-1, peers_all).astype(F32).astype(BF16), NT)
    table_ref[...] = picked[:1].astype(jnp.int32)
    to_scalar = pltpu.make_async_copy(table_ref, table, t_sem)
    to_scalar.start()
    for k in colours:
        arrived(k, (2, None, 2))
        for t in (-1, 1):
            cross(k, 2, t)
    for r in (-1, 1, 2):
        for k in colours:
            arrived_far(k, (2, None, r))
            cross(k, r, 2)
    for copy, arrival in crossings:
        arrival.wait_recv()
    to_scalar.wait()
    load_m.wait()
    load_v.wait()
    far_slots = far_ref.shape[1]
    inner_ref[...] = jnp.zeros_like(inner_ref)

    def far(leaf, carry):
        total = jnp.zeros((rhs, terms), F32)
        for pair in range(far_slots // 2):
            sources, steps = [], []
            for e in (2 * pair, 2 * pair + 1):
                f = far_ref[leaf, e]
                sender = lax.shift_right_logical(f, 2)
                slot = f & 3
                unit = lax.min(lax.max(table[0, sender * 8 + slot], 0), leaves - 1) * 2
                live = lax.min(lax.max(table[0, sender * 8 + 4] - slot, 0), 1)
                which = classes - live * (classes - class_ref[leaf, e])
                place_x = lax.shift_right_logical(sender, 5)
                place_c = lax.shift_right_logical(sender, 4) & 1
                place_y = lax.shift_right_logical(sender, 2) & 3
                place_z = sender & 3
                sources.append(
                    jnp.concatenate(
                        [
                            all_ref[place_x, place_c, place_y, place_z, unit],
                            all_ref[place_x, place_c, place_y, place_z, unit + 1],
                        ],
                        axis=0,
                    )
                )
                steps.append(mats[which])
            total = total + dot(
                jnp.concatenate(sources, axis=1), jnp.concatenate(steps, axis=0)
            )
        lanes = pl.ds(pl.multiple_of(leaf * panels, panels), panels)
        image = base_ref[:, lanes] + dot(total.astype(BF16), pbuf[leaf], NT)
        base_ref[:, lanes] = image
        both = jnp.concatenate(halves(image), axis=0)
        out = dot(both, vbuf[:, :, lanes].reshape(blocks * rhs, panels), NT)
        inner_ref[...] += out[:rhs] + out[rhs:]
        return carry

    lax.fori_loop(0, leaves, far, 0)
    columns = leaves * panels
    def send_to(src, dst, send, recv, peer):
        return pltpu.make_async_remote_copy(
            src_ref=src, dst_ref=dst, send_sem=send, recv_sem=recv,
            device_id=peer, device_id_type=MESH,
        )

    def all_reduce(n, source, arrivals, mine, parts, result):
        rows = rhs // gx
        sent = []
        for by in range(1, gx):
            c, peer = col_peer(by)
            at = pl.ds(pl.multiple_of(c * rows, rows), rows)
            copy = send_to(source.at[at], arrivals.at[gx - by], s1.at[n, by], r1.at[n, gx - by], peer)
            copy.start()
            sent.append(copy)
        own = pl.ds(pl.multiple_of(column * rows, rows), rows)
        total = source[own, :]
        for by in range(1, gx):
            send_to(arrivals.at[by], arrivals.at[by], s1.at[n, by], r1.at[n, by], col_peer(1)[1]).wait_recv()
            total = total + arrivals[by]
        for n_axis, axis in enumerate(("y", "z")):
            slot = mine.at[n_axis]
            slot[...] = total
            for by in range(1, 4):
                i = n_axis * 4 + by
                copy = send_to(
                    slot, parts.at[n_axis * 4 + me[axis]],
                    s2.at[n, i], r2.at[n, n_axis * 4 + 4 - by], line_peer(axis, by)[1],
                )
                copy.start()
                sent.append(copy)
            parts[n_axis * 4 + me[axis]] = total
            for by in range(1, 4):
                c, peer = line_peer(axis, by)
                i = n_axis * 4 + by
                send_to(slot, parts.at[n_axis * 4 + c], s2.at[n, i], r2.at[n, i], peer).wait_recv()
            total = parts[n_axis * 4]
            for c in range(1, 4):
                total = total + parts[n_axis * 4 + c]
        result[own, :] = total
        for by in range(1, gx):
            c, peer = col_peer(by)
            copy = send_to(result.at[own], result.at[own], s3.at[n, by], r3.at[n, gx - by], peer)
            copy.start()
            sent.append(copy)
        for by in range(1, gx):
            c, peer = col_peer(by)
            at = pl.ds(pl.multiple_of(c * rows, rows), rows)
            send_to(result.at[at], result.at[at], s3.at[n, by], r3.at[n, by], peer).wait_recv()
        for copy in sent:
            copy.wait_send()

    scale = 1.0 / total_rows
    all_reduce(0, inner_ref, one_in, piece, two_in, whole)
    proj = whole[...] * scale
    coef = jnp.concatenate(halves(proj), axis=0)
    step = 512
    gram = jnp.zeros((2 * rhs, 2 * rhs), F32)
    for i in range(0, columns, step):
        v = vbuf[:, :, i : i + step].reshape(blocks * rhs, step)
        out = dot(coef, v)
        resid = base_ref[:, i : i + step] - (out[:rhs] + out[rhs:])
        both = jnp.concatenate(halves(resid), axis=0)
        stack[:, i : i + step] = both
        gram = gram + dot(both, both, NT)
    gram_in[...] = gram[:rhs] + gram[rhs:]
    for i in range(0, blocks * rhs, 2 * rhs):
        proj_ref[i : i + 2 * rhs, :] = proj[:, i : i + 2 * rhs].T
    all_reduce(1, gram_in, gone, narrow, two_gone, gram_out)
    folded = gram_out[...] * scale
    folded = folded + pltpu.roll(folded, rhs, 1)
    lane = lax.broadcasted_iota(jnp.int32, (rhs, 2 * rhs), 1)
    row = lax.broadcasted_iota(jnp.int32, (rhs, 2 * rhs), 0)
    work = jnp.where(lane < rhs, folded, (lane - rhs == row).astype(F32))
    tall = 8
    count = rhs // tall
    part = [work[i * tall : (i + 1) * tall] for i in range(count)]
    low = lax.broadcasted_iota(jnp.int32, (tall, 2 * rhs), 0)
    for b in range(count):
        cols = [
            {i: jnp.broadcast_to(part[i][:, b * tall + t : b * tall + t + 1], (tall, 2 * rhs)) for i in range(b, count)}
            for t in range(tall)
        ]
        for t in range(tall):
            inverse = 1.0 / cols[t][b][t : t + 1, :]
            across = {u: cols[u][b][t : t + 1, :] * inverse for u in range(t + 1, tall)}
            pivot = part[b][t : t + 1, :] * inverse
            for i in range(b, count):
                factor = cols[t][i]
                if i == b:
                    factor = jnp.where(low > t, factor, 0.0)
                part[i] = part[i] - factor * pivot
                for u in range(t + 1, tall):
                    cols[u][i] = cols[u][i] - factor * across[u]
    work = jnp.concatenate(part, axis=0)
    diagonal = jnp.sum(jnp.where(lane == row, work, 0.0), axis=1, keepdims=True)
    work = work * lax.rsqrt(diagonal)
    factor_ref[...] = jnp.where((lane >= row) & (lane < rhs), work, 0.0).T[:rhs]
    right = jnp.where(lane < rhs, 0.0, work)
    right = right + pltpu.roll(right, rhs, 1)
    left = jnp.concatenate(halves(right), axis=0)
    for i in range(0, columns, step):
        out = dot(left, stack[:, i : i + step])
        next_ref[:, i : i + step] = (out[:rhs] + out[rhs:]).astype(BF16)
    for copy, arrival in crossings:
        copy.wait_send()
    for copy in started + list_sent:
        copy.wait_send()
    for copy in halo:
        copy.wait_send()


def step(basis, p2m, near_blocks, m2l, send_list, send_count, near_src, near_count, far_src, far_class):
    leaves, slots, panels, _ = near_blocks.shape
    blocks, rhs, columns = basis.shape
    classes, terms = m2l.shape[:2]
    peers = send_list.shape[1]
    units = 2 * leaves
    wide = blocks * rhs
    cuts = (0, 11, 21, units)
    depth = 4
    hbm = pl.BlockSpec(memory_space=pltpu.HBM)
    vmem = pl.BlockSpec(memory_space=pltpu.VMEM)
    smem = pl.BlockSpec(memory_space=pltpu.SMEM)
    dma = pltpu.SemaphoreType.DMA
    return pl.pallas_call(
        functools.partial(step_kernel, cuts, columns * peers),
        in_specs=[hbm, hbm, hbm, hbm, vmem, vmem, smem, smem, smem, smem],
        out_specs=(vmem, vmem, vmem),
        out_shape=(
            jax.ShapeDtypeStruct((rhs, columns), BF16),
            jax.ShapeDtypeStruct((wide, rhs), F32),
            jax.ShapeDtypeStruct((rhs, rhs), F32),
        ),
        scratch_shapes=[
            pltpu.VMEM((4, 2, 4, 4, units, rhs // 2, terms), BF16),
            pltpu.VMEM((3 * leaves, rhs, panels), BF16),
            pltpu.VMEM((depth, slots, panels, panels), BF16),
            pltpu.VMEM((leaves, panels, terms), BF16),
            pltpu.VMEM((units, rhs // 2, terms), BF16),
            pltpu.VMEM((8, peers), jnp.int32),
            pltpu.VMEM((4, 2, 4, 4, 8, peers), jnp.int32),
            pltpu.VMEM((rhs, columns), F32),
            pltpu.VMEM((blocks, rhs, columns), BF16),
            pltpu.VMEM((classes + 1, terms, terms), BF16),
            pltpu.VMEM((1, peers * 8), jnp.int32),
            pltpu.SMEM((1, peers * 8), jnp.int32),
            pltpu.VMEM((rhs, wide), F32),
            pltpu.VMEM((rhs, 2 * rhs), F32),
            pltpu.VMEM((8, 8, wide), F32),
            pltpu.VMEM((8, 8, wide), F32),
            pltpu.VMEM((2 * rhs, columns), BF16),
            pltpu.VMEM((2, 8, wide), F32),
            pltpu.VMEM((rhs, wide), F32),
            pltpu.VMEM((8, 8, 2 * rhs), F32),
            pltpu.VMEM((2, 8, 2 * rhs), F32),
            pltpu.VMEM((8, 8, 2 * rhs), F32),
            pltpu.VMEM((rhs, 2 * rhs), F32),
            dma((2, 8)), dma((2, 8)), dma((2, 8)), dma((2, 8)), dma((2, 8)), dma((2, 8)),
            dma, dma, dma,
            dma((3, 12, 4)), dma((3, 12, 4)), dma((3, 16)), dma((3, 16)),
            dma((2,)), dma((2,)), dma((4, 3)), dma((4, 3)),
            dma, dma, dma, dma, dma((depth,)),
        ],
        compiler_params=pltpu.CompilerParams(
            collective_id=0, has_side_effects=True, vmem_limit_bytes=LIMIT - (896 << 10)
        ),
        name="step",
    )(
        basis, p2m, near_blocks, m2l, jnp.swapaxes(send_list, 1, 2), send_count,
        near_src.T, near_count, far_src, far_class,
    )


def shards(
    basis, near_blocks, near_src, near_count, p2m, m2l, send_list, send_count, far_src, far_class
):
    blocks, rhs, columns = basis.shape
    new, proj, factor = step(
        basis, p2m, near_blocks, m2l, send_list, send_count, near_src, near_count, far_src, far_class
    )
    return (new, proj.reshape(blocks, rhs, rhs), factor)


def solution(mesh):
    finer = Mesh(mesh.devices.reshape(4, 2, 4, 4), ALL)
    in_specs = (
        P(None, None, ALL),
        P(ALL, None, None, None),
        P(ALL, None),
        P(ALL),
        P(ALL, None, None),
        P(),
        P(ALL, None, None),
        P(ALL, None),
        P(ALL, None),
        P(ALL, None),
    )
    out_specs = (P(None, ALL), P(), P())
    return jax.shard_map(
        shards, mesh=finer, in_specs=in_specs, out_specs=out_specs, check_vma=False
    )
```

time: 153 us -> 138 us (0.902)
  Pallas kernels: 147 us -> 132 us
    pallas_call x3 -> x1, Pallas kernels: 147 us -> 132 us  [step(): pl.pallas_call(functools.partial(step_kernel, cuts, columns * peers), in_...]
where the time goes in v4:
time: 138 us; the launch traced here: 137 us
  Pallas kernels  132 us (96%)
  local copies, waits for them, and re-layouts  4.91 us (4%)
    pallas_call x1, Pallas kernels, step(): pl.pallas_call(functools.partial(step_kernel, cuts, columns * peers), in_...  132 us
    unnamed x3, local copies, waits for them, and re-layouts  4.91 us

profile of v4, /device:TPU:1, one launch (start us, length us, event | category | flops | bytes accessed | tf_op | source)
XLA Modules:
  0.0 137.5 jit_solution(16363186978453895045)
XLA Ops:
  0.6 131.9 %step.1 = (bf16[64,4096]{1,0:T(8,128)(2,1)}, f32[512,64]{1,0:T(8,128)}, f32[64,64]{1,0:T(8,128)}) custom-call(bf16[8,64,4096]{2,1,0:T(8,128)(2,1)} %basis_ref.1, bf16[16,256,128]{2,1,0:T(8,128)(2,1)} %p_ref.1, bf16[16,8,256,256]{3,2,1,0:T(8,128)(2,1)} %near_blocks_ref.1, bf16[16,128,128]{2,1,0:T(8,128)(2,1)} %m2l_ref.1, s32[1,4,128]{2,1,0:T(4,128)} %bitcast.5, ...), custom_call_target="tpu_custom_call" | custom-call | tf_op jit(solution)/shard_map/step/pallas_call | solution.py:544
  132.5 1.9 %copy.16 = bf16[64,4096]{1,0:T(8,128)(2,1)} copy(bf16[64,4096]{1,0:T(8,128)(2,1)} %get-tuple-element.12) | data formatting | bytes 1048576
  134.4 1.7 %copy.17 = f32[8,64,64]{2,1,0:T(8,128)} copy(f32[8,64,64]{2,1,0:T(8,128)} %bitcast.3) | data formatting | bytes 262144
  136.1 1.4 copy.18

commit v5 on v4

--- a/solution.py
+++ b/solution.py
@@ -29,8 +29,8 @@
 def step_kernel(
     cuts, total_rows, basis_ref, p_ref, near_blocks_ref, m2l_ref, list_ref, count_ref,
     src_ref, near_count_ref, far_ref, class_ref,
-    next_ref, proj_ref, factor_ref,
-    all_ref, xbuf, nbuf, pbuf, mbuf, stage, lists, base_ref, vbuf, mats, table_ref, table,
+    stack_ref, proj_ref, left_ref, factor_ref,
+    proj_buf, out_sem, all_ref, xbuf, nbuf, pbuf, mbuf, stage, lists, base_ref, vbuf, mats, table_ref, table,
     inner_ref, gram_in, one_in, two_in, stack, piece, whole, gone, narrow, two_gone, gram_out,
     s1, r1, s2, r2, s3, r3, v_sem, m_sem, t_sem,
     send_sem, recv_sem, sib_send, sib_recv, halo_send, halo_recv, list_send, list_recv,
@@ -378,7 +378,9 @@
     far_slots = far_ref.shape[1]
     inner_ref[...] = jnp.zeros_like(inner_ref)
 
-    def far(leaf, carry):
+    group = 4
+
+    def expansion(leaf):
         total = jnp.zeros((rhs, terms), F32)
         for pair in range(far_slots // 2):
             sources, steps = [], []
@@ -406,15 +408,22 @@
             total = total + dot(
                 jnp.concatenate(sources, axis=1), jnp.concatenate(steps, axis=0)
             )
-        lanes = pl.ds(pl.multiple_of(leaf * panels, panels), panels)
-        image = base_ref[:, lanes] + dot(total.astype(BF16), pbuf[leaf], NT)
-        base_ref[:, lanes] = image
-        both = jnp.concatenate(halves(image), axis=0)
-        out = dot(both, vbuf[:, :, lanes].reshape(blocks * rhs, panels), NT)
+        return total.astype(BF16)
+
+    def far(g, carry):
+        first = g * group
+        local = [expansion(first + j) for j in range(group)]
+        for j in range(group):
+            lanes = pl.ds(pl.multiple_of((first + j) * panels, panels), panels)
+            base_ref[:, lanes] += dot(local[j], pbuf[first + j], NT)
+        width = group * panels
+        lanes = pl.ds(pl.multiple_of(g * width, width), width)
+        both = jnp.concatenate(halves(base_ref[:, lanes]), axis=0)
+        out = dot(both, vbuf[:, :, lanes].reshape(blocks * rhs, width), NT)
         inner_ref[...] += out[:rhs] + out[rhs:]
         return carry
 
-    lax.fori_loop(0, leaves, far, 0)
+    lax.fori_loop(0, leaves // group, far, 0)
     columns = leaves * panels
     def send_to(src, dst, send, recv, peer):
         return pltpu.make_async_remote_copy(
@@ -483,7 +492,13 @@
         gram = gram + dot(both, both, NT)
     gram_in[...] = gram[:rhs] + gram[rhs:]
     for i in range(0, blocks * rhs, 2 * rhs):
-        proj_ref[i : i + 2 * rhs, :] = proj[:, i : i + 2 * rhs].T
+        proj_buf[i : i + 2 * rhs, :] = proj[:, i : i + 2 * rhs].T
+    leaving = [
+        pltpu.make_async_copy(stack, stack_ref, out_sem.at[0]),
+        pltpu.make_async_copy(proj_buf, proj_ref, out_sem.at[1]),
+    ]
+    for copy in leaving:
+        copy.start()
     all_reduce(1, gram_in, gone, narrow, two_gone, gram_out)
     folded = gram_out[...] * scale
     folded = folded + pltpu.roll(folded, rhs, 1)
@@ -516,10 +531,9 @@
     factor_ref[...] = jnp.where((lane >= row) & (lane < rhs), work, 0.0).T[:rhs]
     right = jnp.where(lane < rhs, 0.0, work)
     right = right + pltpu.roll(right, rhs, 1)
-    left = jnp.concatenate(halves(right), axis=0)
-    for i in range(0, columns, step):
-        out = dot(left, stack[:, i : i + step])
-        next_ref[:, i : i + step] = (out[:rhs] + out[rhs:]).astype(BF16)
+    left_ref[...] = jnp.concatenate(halves(right), axis=0)
+    for copy in leaving:
+        copy.wait()
     for copy, arrival in crossings:
         copy.wait_send()
     for copy in started + list_sent:
@@ -544,13 +558,16 @@
     return pl.pallas_call(
         functools.partial(step_kernel, cuts, columns * peers),
         in_specs=[hbm, hbm, hbm, hbm, vmem, vmem, smem, smem, smem, smem],
-        out_specs=(vmem, vmem, vmem),
+        out_specs=(hbm, hbm, vmem, vmem),
         out_shape=(
-            jax.ShapeDtypeStruct((rhs, columns), BF16),
+            jax.ShapeDtypeStruct((2 * rhs, columns), BF16),
             jax.ShapeDtypeStruct((wide, rhs), F32),
+            jax.ShapeDtypeStruct((2 * rhs, 2 * rhs), BF16),
             jax.ShapeDtypeStruct((rhs, rhs), F32),
         ),
         scratch_shapes=[
+            pltpu.VMEM((wide, rhs), F32),
+            dma((2,)),
             pltpu.VMEM((4, 2, 4, 4, units, rhs // 2, terms), BF16),
             pltpu.VMEM((3 * leaves, rhs, panels), BF16),
             pltpu.VMEM((depth, slots, panels, panels), BF16),
@@ -581,7 +598,7 @@
             dma, dma, dma, dma, dma((depth,)),
         ],
         compiler_params=pltpu.CompilerParams(
-            collective_id=0, has_side_effects=True, vmem_limit_bytes=LIMIT - (896 << 10)
+            collective_id=0, has_side_effects=True, vmem_limit_bytes=LIMIT
         ),
         name="step",
     )(
@@ -590,13 +607,54 @@
     )
 
 
+def last_kernel(stack_ref, proj_in, left_ref, factor_in, next_ref, proj_ref, factor_ref):
+    rhs = next_ref.shape[0]
+
+    @pl.when(pl.program_id(0) == 0)
+    def _():
+        proj_ref[...] = proj_in[...]
+        factor_ref[...] = factor_in[...]
+
+    out = dot(left_ref[...], stack_ref[...])
+    next_ref[...] = (out[:rhs] + out[rhs:]).astype(BF16)
+
+
+def last(stack, proj, left, factor):
+    double, columns = stack.shape
+    rhs = double // 2
+    steps = 4
+
+    def fixed(array):
+        return pl.BlockSpec(array.shape, lambda i: (0, 0))
+
+    return pl.pallas_call(
+        last_kernel,
+        grid=(steps,),
+        in_specs=[
+            pl.BlockSpec((double, columns // steps), lambda i: (0, i)),
+            fixed(proj), fixed(left), fixed(factor),
+        ],
+        out_specs=(
+            pl.BlockSpec((rhs, columns // steps), lambda i: (0, i)), fixed(proj), fixed(factor),
+        ),
+        out_shape=(
+            jax.ShapeDtypeStruct((rhs, columns), BF16),
+            jax.ShapeDtypeStruct(proj.shape, F32),
+            jax.ShapeDtypeStruct(factor.shape, F32),
+        ),
+        compiler_params=pltpu.CompilerParams(vmem_limit_bytes=LIMIT),
+        name="last",
+    )(stack, proj, left, factor)
+
+
 def shards(
     basis, near_blocks, near_src, near_count, p2m, m2l, send_list, send_count, far_src, far_class
 ):
     blocks, rhs, columns = basis.shape
-    new, proj, factor = step(
+    stack, proj, left, factor = step(
         basis, p2m, near_blocks, m2l, send_list, send_count, near_src, near_count, far_src, far_class
     )
+    new, proj, factor = last(stack, proj, left, factor)
     return (new, proj.reshape(blocks, rhs, rhs), factor)
 
 

time: 138 us -> 133 us (0.964)
  local copies, waits for them, and re-layouts: 4.91 us -> 0 us
    unnamed x3 -> x0, local copies, waits for them, and re-layouts: 4.91 us -> none
    pallas_call x0 -> x1, Pallas kernels: none -> 3.83 us  [last(): pl.pallas_call(last_kernel, grid=(steps,), in_specs=[pl.BlockSpec((double...]
    pallas_call x1, Pallas kernels: 132 us -> 128 us  [step(): pl.pallas_call(functools.partial(step_kernel, cuts, columns * peers), in_...]
where the time goes in v5:
time: 133 us
  Pallas kernels  132 us (99%)
    pallas_call x1, Pallas kernels, step(): pl.pallas_call(functools.partial(step_kernel, cuts, columns * peers), in_...  128 us
    pallas_call x1, Pallas kernels, last(): pl.pallas_call(last_kernel, grid=(steps,), in_specs=[pl.BlockSpec((double...  3.83 us

profile of v5, /device:TPU:1, one launch (start us, length us, event | category | flops | bytes accessed | tf_op | source)
XLA Modules:
  0.0 132.9 jit_solution(4717623517827021641)
XLA Ops:
  0.6 128.4 %step.1 = (bf16[128,4096]{1,0:T(8,128)(2,1)}, f32[512,64]{1,0:T(8,128)}, bf16[128,128]{1,0:T(8,128)(2,1)}, f32[64,64]{1,0:T(8,128)}) custom-call(bf16[8,64,4096]{2,1,0:T(8,128)(2,1)} %basis_ref.1, bf16[16,256,128]{2,1,0:T(8,128)(2,1)} %p_ref.1, bf16[16,8,256,256]{3,2,1,0:T(8,128)(2,1)} %near_blocks_ref.1, bf16[16,128,128]{2,1,0:T(8,128)(2,1)} %m2l_ref.1, ...), custom_call_target="tpu_custom_call" | custom-call | tf_op jit(solution)/shard_map/step/pallas_call | solution.py:558
  129.0 3.8 %last.1 = (bf16[64,4096]{1,0:T(8,128)(2,1)}, f32[512,64]{1,0:T(8,128)}, f32[64,64]{1,0:T(8,128)}) custom-call(bf16[128,4096]{1,0:T(8,128)(2,1)} %get-tuple-element.10.stack_ref, f32[512,64]{1,0:T(8,128)} %get-tuple-element.11.proj_in, bf16[128,128]{1,0:T(8,128)(2,1)} %get-tuple-element.12.left_ref, f32[64,64]{1,0:T(8,128)} %get-tuple-element.13.factor_in), custom_call_target="tpu_custom_call" | custom-call | tf_op jit(solution)/shard_map/last/pallas_call | solution.py:630

commit v6 on v5

--- a/solution.py
+++ b/solution.py
@@ -378,7 +378,9 @@
     far_slots = far_ref.shape[1]
     inner_ref[...] = jnp.zeros_like(inner_ref)
 
-    group = 4
+    group = 8
+
+    flat_ref = all_ref.reshape(-1, rhs // 2, terms)
 
     def expansion(leaf):
         total = jnp.zeros((rhs, terms), F32)
@@ -391,15 +393,12 @@
                 unit = lax.min(lax.max(table[0, sender * 8 + slot], 0), leaves - 1) * 2
                 live = lax.min(lax.max(table[0, sender * 8 + 4] - slot, 0), 1)
                 which = classes - live * (classes - class_ref[leaf, e])
-                place_x = lax.shift_right_logical(sender, 5)
-                place_c = lax.shift_right_logical(sender, 4) & 1
-                place_y = lax.shift_right_logical(sender, 2) & 3
-                place_z = sender & 3
+                spot = sender * (2 * leaves) + unit
                 sources.append(
                     jnp.concatenate(
                         [
-                            all_ref[place_x, place_c, place_y, place_z, unit],
-                            all_ref[place_x, place_c, place_y, place_z, unit + 1],
+                            flat_ref[spot],
+                            flat_ref[spot + 1],
                         ],
                         axis=0,
                     )
@@ -431,10 +430,11 @@
             device_id=peer, device_id_type=MESH,
         )
 
-    def all_reduce(n, source, arrivals, mine, parts, result):
+    def all_reduce(n, source, arrivals, mine, parts, result, meanwhile=None):
         rows = rhs // gx
+        far_first = (4, 5, 3, 6, 2, 7, 1)
         sent = []
-        for by in range(1, gx):
+        for by in far_first:
             c, peer = col_peer(by)
             at = pl.ds(pl.multiple_of(c * rows, rows), rows)
             copy = send_to(source.at[at], arrivals.at[gx - by], s1.at[n, by], r1.at[n, gx - by], peer)
@@ -442,13 +442,15 @@
             sent.append(copy)
         own = pl.ds(pl.multiple_of(column * rows, rows), rows)
         total = source[own, :]
+        if meanwhile is not None:
+            meanwhile()
         for by in range(1, gx):
             send_to(arrivals.at[by], arrivals.at[by], s1.at[n, by], r1.at[n, by], col_peer(1)[1]).wait_recv()
             total = total + arrivals[by]
         for n_axis, axis in enumerate(("y", "z")):
             slot = mine.at[n_axis]
             slot[...] = total
-            for by in range(1, 4):
+            for by in (2, 1, 3):
                 i = n_axis * 4 + by
                 copy = send_to(
                     slot, parts.at[n_axis * 4 + me[axis]],
@@ -465,7 +467,7 @@
             for c in range(1, 4):
                 total = total + parts[n_axis * 4 + c]
         result[own, :] = total
-        for by in range(1, gx):
+        for by in far_first:
             c, peer = col_peer(by)
             copy = send_to(result.at[own], result.at[own], s3.at[n, by], r3.at[n, gx - by], peer)
             copy.start()
@@ -491,15 +493,18 @@
         stack[:, i : i + step] = both
         gram = gram + dot(both, both, NT)
     gram_in[...] = gram[:rhs] + gram[rhs:]
-    for i in range(0, blocks * rhs, 2 * rhs):
-        proj_buf[i : i + 2 * rhs, :] = proj[:, i : i + 2 * rhs].T
     leaving = [
         pltpu.make_async_copy(stack, stack_ref, out_sem.at[0]),
         pltpu.make_async_copy(proj_buf, proj_ref, out_sem.at[1]),
     ]
-    for copy in leaving:
-        copy.start()
-    all_reduce(1, gram_in, gone, narrow, two_gone, gram_out)
+
+    def hand_out():
+        for i in range(0, blocks * rhs, 2 * rhs):
+            proj_buf[i : i + 2 * rhs, :] = proj[:, i : i + 2 * rhs].T
+        for copy in leaving:
+            copy.start()
+
+    all_reduce(1, gram_in, gone, narrow, two_gone, gram_out, hand_out)
     folded = gram_out[...] * scale
     folded = folded + pltpu.roll(folded, rhs, 1)
     lane = lax.broadcasted_iota(jnp.int32, (rhs, 2 * rhs), 1)
@@ -549,7 +554,7 @@
     peers = send_list.shape[1]
     units = 2 * leaves
     wide = blocks * rhs
-    cuts = (0, 11, 21, units)
+    cuts = (0, 11, 20, units)
     depth = 4
     hbm = pl.BlockSpec(memory_space=pltpu.HBM)
     vmem = pl.BlockSpec(memory_space=pltpu.VMEM)
@@ -622,7 +627,7 @@
 def last(stack, proj, left, factor):
     double, columns = stack.shape
     rhs = double // 2
-    steps = 4
+    steps = 2
 
     def fixed(array):
         return pl.BlockSpec(array.shape, lambda i: (0, 0))

time: 133 us -> 127 us (0.955)
  Pallas kernels: 132 us -> 126 us
    pallas_call x1, Pallas kernels: 128 us -> 124 us  [step(): pl.pallas_call(functools.partial(step_kernel, cuts, columns * peers), in_...]
    pallas_call x1, Pallas kernels: 3.83 us -> 2.48 us  [last(): pl.pallas_call(last_kernel, grid=(steps,), in_specs=[pl.BlockSpec((double...]
where the time goes in v6:
time: 127 us
  Pallas kernels  126 us (99%)
    pallas_call x1, Pallas kernels, step(): pl.pallas_call(functools.partial(step_kernel, cuts, columns * peers), in_...  124 us

profile of v6, /device:TPU:1, one launch (start us, length us, event | category | flops | bytes accessed | tf_op | source)
XLA Modules:
  0.0 126.7 jit_solution(4822260539421611807)
XLA Ops:
  0.6 123.6 %step.1 = (bf16[128,4096]{1,0:T(8,128)(2,1)}, f32[512,64]{1,0:T(8,128)}, bf16[128,128]{1,0:T(8,128)(2,1)}, f32[64,64]{1,0:T(8,128)}) custom-call(bf16[8,64,4096]{2,1,0:T(8,128)(2,1)} %basis_ref.1, bf16[16,256,128]{2,1,0:T(8,128)(2,1)} %p_ref.1, bf16[16,8,256,256]{3,2,1,0:T(8,128)(2,1)} %near_blocks_ref.1, bf16[16,128,128]{2,1,0:T(8,128)(2,1)} %m2l_ref.1, ...), custom_call_target="tpu_custom_call" | custom-call | tf_op jit(solution)/shard_map/step/pallas_call | solution.py:563
  124.2 2.5 %last.1 = (bf16[64,4096]{1,0:T(8,128)(2,1)}, f32[512,64]{1,0:T(8,128)}, f32[64,64]{1,0:T(8,128)}) custom-call(bf16[128,4096]{1,0:T(8,128)(2,1)} %get-tuple-element.10.stack_ref, f32[512,64]{1,0:T(8,128)} %get-tuple-element.11.proj_in, bf16[128,128]{1,0:T(8,128)(2,1)} %get-tuple-element.12.left_ref, f32[64,64]{1,0:T(8,128)} %get-tuple-element.13.factor_in), custom_call_target="tpu_custom_call" | custom-call | tf_op jit(solution)/shard_map/last/pallas_call | solution.py:635
